TPU v7x, 32 devices: a whole 2x2x4 slice. The times are simulated.
32 devices in a mesh: gx: 4 (over z), gy: 4 (over y, x), gz: 2 (over core).
Axes of the slice: x: 2, y: 2, z: 4, core: 2. Of those that a mesh axis runs over, the one named last changes fastest.
Arguments:
- offsets: float32 [3, 131072], P(None, ('gx', 'gy', 'gz')), may hold values from 0 to 1
- strength: float32 [3, 131072], P(None, ('gx', 'gy', 'gz')), may hold values from -0.012 to 0.012
- ghost_list: int32 [49152], P(('gx', 'gy', 'gz')), may hold values from 0 to 4095
- pair_targets: int32 [4096], P(('gx', 'gy', 'gz')), may hold values from 0 to 31
- pair_sources: int32 [4096], P(('gx', 'gy', 'gz')), may hold values from 0 to 103
- owners: int32 [1024, 1], P(('gx', 'gy', 'gz')), may hold values from 0 to 15; in each aligned block of 32 rows (0 to 31, 32 to 63, ...) at most 4 rows name the same one
Outputs:
- moved_positions: float32 [2048, 3, 128], P(('gx', 'gy', 'gz'))
- moved_velocity: float32 [2048, 3, 128], P(('gx', 'gy', 'gz'))
Inputs may be any that keep to these rules, and one draw needn't show every extreme that they name: `owners`: among the 32 blocks of one domain no owner is named more than 4 times.
All inputs are finite; a program needn't handle non-finite values.
Results may differ from a plain program's by a relative error of at most 0.0003.
Values sent between devices are 32-bit elements; how exact they have to be, the bound alone decides.
No kernel may reach another device: no remote copies, remote signals or barrier semaphores. Data moves between devices by JAX's collectives and lax.ppermute only.
A program may use at most 128 MiB of HBM per device.

v0:
```python
import functools
import math

import jax
import jax.numpy as jnp
import numpy as np
from jax import lax
from jax.experimental import pallas as pl
from jax.experimental.pallas import tpu as pltpu
from jax.sharding import PartitionSpec as P

ORDER = 5
LANES = 128
ROWS = 8
FEATURES = 32
BATCH = 16

core_sq = 0.0025
time_step = 0.1
everywhere = ("gx", "gy", "gz")
f32 = jnp.float32
bf16 = jnp.bfloat16


def exponents():
    entries = []
    for degree in range(ORDER + 1):
        for leading in range(degree, -1, -1):
            for middle in range(degree - leading, -1, -1):
                entries.append((leading, middle, degree - leading - middle))
    return entries


POWERS = exponents()
TERMS = len(POWERS)
PLACE = {triple: spot for spot, triple in enumerate(POWERS)}
FACTORIAL = [float(np.prod([math.factorial(e) for e in triple])) for triple in POWERS]


def row_ids():
    return lax.broadcasted_iota(jnp.int32, (ROWS, LANES), 0)


def spread(ref, row):
    return ref[pl.ds(row, ROWS, stride=0), :]


def tile_of(ref, tile):
    return ref[pl.ds(pl.multiple_of(tile * ROWS, ROWS), ROWS), :]


def slab_middle(deep):
    side_z = 1.0 / deep
    middle_x = lax.axis_index("gx").astype(f32) + 0.5
    middle_y = lax.axis_index("gy").astype(f32) + 0.5
    middle_z = lax.axis_index("gz").astype(f32) * side_z + 0.5 * side_z
    return middle_x, middle_y, middle_z


def relative_pair(pack, pair, middle):
    low = row_ids() < 4
    base = pair * (2 * ROWS)
    return [
        jnp.where(low, spread(pack, base + axis), spread(pack, base + ROWS + axis)) - middle[axis]
        for axis in range(3)
    ]


def leaf_moments(pack, tiles, devices, leaf, work, line):
    middle_x, middle_y, _ = slab_middle(1)
    middle = (middle_x, middle_y, 0.5)
    low = row_ids() < 4

    def accumulate(chosen):
        def body(pair, sums):
            x, y, z = relative_pair(pack, pair, middle)
            even, odd = tile_of(pack, 2 * pair), tile_of(pack, 2 * pair + 1)
            first = jnp.where(low, pltpu.roll(even, 4, 0), odd)
            value = {(0, 0, 0): first}
            gained = []
            for a in range(ORDER + 1):
                if a > 0:
                    value[a, 0, 0] = value[a - 1, 0, 0] * x
                if a not in chosen:
                    continue
                for b in range(ORDER + 1 - a):
                    if b > 0:
                        value[a, b, 0] = value[a, b - 1, 0] * y
                    for c in range(ORDER + 1 - a - b):
                        if c > 0:
                            value[a, b, c] = value[a, b, c - 1] * z
                        gained.append(value[a, b, c])
            return tuple(total + more for total, more in zip(sums, gained))

        names = [
            (a, b, c)
            for a in chosen
            for b in range(ORDER + 1 - a)
            for c in range(ORDER + 1 - a - b)
        ]
        zero = jnp.zeros((ROWS, LANES), f32)
        sums = lax.fori_loop(0, tiles // 2, body, tuple(zero for _ in names))
        for name, total in zip(names, sums):
            spot = PLACE[name]
            factor = (-1.0) ** sum(name) / FACTORIAL[spot]
            work[spot * ROWS : (spot + 1) * ROWS, :] = total * factor

    accumulate((0,))
    accumulate((1, 2, 3, 4, 5))
    line[...] = jnp.zeros_like(line)
    for k in range(3):
        both = work[pl.ds(k, TERMS, stride=ROWS), :] + work[pl.ds(k + 4, TERMS, stride=ROWS), :]
        summed = jnp.sum(both.T, axis=0, keepdims=True)
        line[k : k + 1, 0:TERMS] = summed
        line[k + 4 : k + 5, 0:TERMS] = summed
    copies = line[...]
    for at in range(devices * 4 // ROWS):
        leaf[at * ROWS : (at + 1) * ROWS, :] = copies


def pick_ghosts(pack, tiles, ghost_ids, ghosts):
    for out_tile in range(ghost_ids.shape[0]):
        wanted = jnp.broadcast_to(ghost_ids[out_tile : out_tile + 1, :], (ROWS, LANES))
        lane, owner = wanted & (LANES - 1), wanted >> 7
        found = jnp.zeros((ROWS, LANES), f32)
        for tile in range(tiles):
            moved = jnp.take_along_axis(
                pack[tile * ROWS : (tile + 1) * ROWS, :], lane, axis=1, mode="promise_in_bounds"
            )
            found = jnp.where(owner == tile, moved, found)
        ghosts[out_tile * ROWS : (out_tile + 1) * ROWS, :] = found


def prologue_kernel(tiles, devices, deep, offsets, strength, ghost_ids, pack, leaf, ghosts, work, line):
    side_z = 1.0 / deep
    axis = lax.broadcasted_iota(jnp.int32, (3, LANES), 0)
    corner = jnp.where(
        axis == 0,
        lax.axis_index("gx").astype(f32),
        jnp.where(
            axis == 1, lax.axis_index("gy").astype(f32), lax.axis_index("gz").astype(f32) * side_z
        ),
    )
    sides = jnp.where(axis == 2, side_z, 1.0)
    blank = jnp.zeros((1, LANES), f32)
    for tile in range(tiles):
        span = slice(tile * LANES, (tile + 1) * LANES)
        base = tile * ROWS
        pack[base : base + 3, :] = corner + offsets[:, span] * sides
        pack[base + 3 : base + 4, :] = blank
        pack[base + 4 : base + 7, :] = strength[:, span]
        pack[base + 7 : base + 8, :] = blank
    leaf_moments(pack, tiles, devices, leaf, work, line)
    pick_ghosts(pack, tiles, ghost_ids, ghosts)


def derivative_kernel(wide, tall, deep, table):
    lane = lax.broadcasted_iota(jnp.int32, (ROWS, LANES), 1)
    column_x = jnp.zeros((ROWS, LANES), jnp.int32)
    for step in range(1, wide):
        column_x = column_x + (lane >= step * tall).astype(jnp.int32)
    column_y = lane - column_x * tall
    gap_x = lax.axis_index("gx") - column_x
    gap_y = lax.axis_index("gy") - column_y
    far = (jnp.maximum(jnp.abs(gap_x), jnp.abs(gap_y)) >= 3) & (lane < wide * tall)
    weight = jnp.where(far, 1.0, 0.0)
    middle_z = slab_middle(deep)[2]
    r = (gap_x.astype(f32), gap_y.astype(f32), jnp.full((ROWS, LANES), middle_z - 0.5, f32))
    square = r[0] * r[0] + r[1] * r[1] + r[2] * r[2] + core_sq
    inverse = 1.0 / square
    taylor = {(0, 0, 0): lax.rsqrt(square)}
    for spot, triple in enumerate(POWERS):
        degree = sum(triple)
        if degree > 0:
            once, twice = None, None
            for axis in range(3):
                down = list(triple)
                down[axis] -= 1
                if down[axis] >= 0:
                    term = r[axis] * taylor[tuple(down)]
                    once = term if once is None else once + term
                down[axis] -= 1
                if down[axis] >= 0:
                    term = taylor[tuple(down)]
                    twice = term if twice is None else twice + term
            total = once * (-(2.0 * degree - 1.0) / degree)
            if twice is not None:
                total = total - twice * ((degree - 1.0) / degree)
            taylor[triple] = total * inverse
        scaled = taylor[triple] * weight * FACTORIAL[spot]
        table[spot : spot + 1, :] = scaled[0:1, :]


def split_three(value):
    first = value.astype(bf16).astype(f32)
    rest = value - first
    second = rest.astype(bf16).astype(f32)
    return first, second, rest - second


def join(upper, lower):
    return jnp.where(row_ids() < 4, upper, pltpu.roll(lower, 4, 0))


def store_features(place, ref, parts):
    ref[pl.ds(pl.multiple_of(place * FEATURES, FEATURES), FEATURES), :] = jnp.concatenate(
        parts, axis=0
    ).astype(bf16)


def squares_in_row_three(value):
    square = value * value
    return pltpu.roll(square, 1, 0) + pltpu.roll(square, 2, 0) + pltpu.roll(square, 3, 0)


def centred(tile, middle):
    row = row_ids()
    shift = jnp.where(row == 0, middle[0], jnp.where(row == 1, middle[1], middle[2]))
    return jnp.where(row < 3, tile - shift, 0.0)


def source_features(tile, middle, place, sources, pushes):
    row = row_ids()
    here = centred(tile, middle)
    here = jnp.where(row == 3, squares_in_row_three(here) + core_sq, here)
    one, two, three = split_three(here)
    ones = jnp.where(row < 3, 1.0, 0.0)
    store_features(place, sources, [join(one, one), join(two, two), join(one, three), ones])
    push = jnp.where(row >= 4, tile, 0.0)
    one, two, three = split_three(push)
    lines = jnp.concatenate([pltpu.roll(one, 4, 0) + two, pltpu.roll(three, 4, 0)], axis=0).astype(bf16)
    spot = pl.ds(pl.multiple_of(place * 2 * ROWS, 2 * ROWS), 2 * ROWS)
    pushes[spot, 0:LANES] = lines
    pushes[spot, LANES : 2 * LANES] = lines


def target_features(tile, middle, place, targets):
    row = row_ids()
    here = centred(tile, middle)
    size = squares_in_row_three(here)
    one, two, three = split_three(jnp.where(row == 3, 1.0, here * -2.0))
    first, second, third = split_three(size)
    sizes = jnp.where(
        row == 0,
        pltpu.roll(first, 5, 0),
        jnp.where(row == 1, pltpu.roll(second, 6, 0), pltpu.roll(third, 7, 0)),
    )
    sizes = jnp.where(row < 3, sizes, 0.0)
    store_features(place, targets, [join(one, two), join(one, two), join(three, one), sizes])


def step_kernel(
    tiles, ghost_tiles, wide, tall, deep, beside, final, capacity,
    pair_targets, pair_sources, owners, pack, received, table, ghost_ids, *rest,
):
    devices = wide * tall * deep
    columns = wide * tall
    ghost_in = rest[: 2 * len(beside)]
    rest = rest[2 * len(beside) :]
    if final:
        sent, pack_out, speed, sources, targets, pushes, near, work, expansion, square, slots, counts = rest
    else:
        pack_out, leaf, ghosts, speed, sources, targets, pushes, near, work, expansion, square, line = rest
    row = row_ids()
    middle = slab_middle(deep)

    square[...] = jnp.zeros_like(square)
    work[...] = jnp.zeros_like(work)
    for k in range(3):
        total = received[pl.ds(k, columns, stride=4 * deep), :]
        for slab in range(1, deep):
            total = total + received[pl.ds(slab * 4 + k, columns, stride=4 * deep), :]
        square[0:columns, :] = total
        turned = square[...].T[0:TERMS, :]
        work[pl.ds(k, TERMS, stride=ROWS), :] = turned
        work[pl.ds(k + 4, TERMS, stride=ROWS), :] = turned
    for spot, outer in enumerate(POWERS):
        total = None
        for inner_spot, inner in enumerate(POWERS):
            if sum(outer) + sum(inner) > ORDER:
                continue
            merged = tuple(o + i for o, i in zip(outer, inner))
            term = spread(table, PLACE[merged]) * work[inner_spot * ROWS : (inner_spot + 1) * ROWS, :]
            total = term if total is None else total + term
        summed = jnp.sum(total, axis=1, keepdims=True) * (1.0 / FACTORIAL[spot])
        expansion[spot * ROWS : (spot + 1) * ROWS, :] = jnp.broadcast_to(summed, (ROWS, LANES))

    def evaluate(pair, carry):
        x, y, z = relative_pair(pack, pair, middle)
        over_x = None
        for a in range(ORDER, -1, -1):
            over_y = None
            for b in range(ORDER - a, -1, -1):
                over_z = None
                for c in range(ORDER - a - b, -1, -1):
                    spot = PLACE[a, b, c]
                    factor = expansion[spot * ROWS : (spot + 1) * ROWS, :]
                    over_z = factor if over_z is None else over_z * z + factor
                over_y = over_z if over_y is None else over_y * y + over_z
            over_x = over_y if over_x is None else over_x * x + over_y
        spot = pl.multiple_of(pair * (2 * ROWS), 2 * ROWS)
        speed[pl.ds(spot, ROWS), :] = over_x
        speed[pl.ds(spot + ROWS, ROWS), :] = pltpu.roll(over_x, 4, 0)
        return carry

    lax.fori_loop(0, tiles // 2, evaluate, 0)

    def own_tile(tile, carry):
        value = tile_of(pack, tile)
        source_features(value, middle, tile, sources, pushes)
        target_features(value, middle, tile, targets)
        return carry

    lax.fori_loop(0, tiles, own_tile, 0, unroll=2)
    for number, (name, count) in enumerate(beside):
        index = lax.axis_index(name)
        odd = lax.rem(index, 2) == 1
        has_lower, has_upper = index > 0, index < count - 1
        from_a, from_b = ghost_in[2 * number], ghost_in[2 * number + 1]

        def ghost_tile(tile, carry, number=number, odd=odd, lows=has_lower, ups=has_upper, a=from_a, b=from_b):
            one, other = tile_of(a, tile), tile_of(b, tile)
            base = tiles + 2 * number * ghost_tiles + tile
            for which, (value, present) in enumerate(
                ((jnp.where(odd, one, other), lows), (jnp.where(odd, other, one), ups))
            ):
                value = jnp.where((row < 4) | present, value, 0.0)
                source_features(value, middle, base + which * ghost_tiles, sources, pushes)
            return carry

        lax.fori_loop(0, ghost_tiles, ghost_tile, 0)

    near[...] = jnp.zeros_like(near)
    pair_count = pair_targets.shape[0]
    batch = BATCH if pair_count % BATCH == 0 else 1

    def batch_of_pairs(number, carry):
        names = [(pair_targets[number * batch + at], pair_sources[number * batch + at]) for at in range(batch)]
        gaps = [
            lax.dot_general(
                sources[pl.ds(pl.multiple_of(there * FEATURES, FEATURES), FEATURES), :],
                targets[pl.ds(pl.multiple_of(here * FEATURES, FEATURES), FEATURES), :],
                (((0,), (0,)), ((), ())),
                preferred_element_type=f32,
            )
            for here, there in names
        ]
        weights = []
        for gap in gaps:
            kernel_block = lax.rsqrt(jnp.maximum(gap, core_sq))
            coarse = kernel_block.astype(bf16)
            fine = (kernel_block - coarse.astype(f32)).astype(bf16)
            weights.append(jnp.concatenate([coarse, fine], axis=0))
        gains = [
            jnp.dot(
                pushes[pl.ds(pl.multiple_of(there * 2 * ROWS, 2 * ROWS), 2 * ROWS), :],
                weight,
                preferred_element_type=f32,
            )
            for (here, there), weight in zip(names, weights)
        ]
        for (here, there), gain in zip(names, gains):
            spot = pl.ds(pl.multiple_of(here * 2 * ROWS, 2 * ROWS), 2 * ROWS)
            near[spot, :] = near[spot, :] + gain
        return carry

    lax.fori_loop(0, pair_count // batch, batch_of_pairs, 0)

    def advance(tile, carry):
        spot = pl.multiple_of(tile * 2 * ROWS, 2 * ROWS)
        upper, lower = near[pl.ds(spot, ROWS), :], near[pl.ds(spot + ROWS, ROWS), :]
        close = upper + pltpu.roll(upper, 4, 0) + lower
        velocity = jnp.where(row < 3, close + tile_of(speed, tile), 0.0)
        place = pl.ds(pl.multiple_of(tile * ROWS, ROWS), ROWS)
        speed[place, :] = velocity
        pack_out[place, :] = pack[place, :] + time_step * velocity
        return carry

    lax.fori_loop(0, tiles, advance, 0, unroll=4)

    if not final:
        leaf_moments(pack_out, tiles, devices, leaf, work, line)
        pick_ghosts(pack_out, tiles, ghost_ids, ghosts)
        return

    group = wide * tall
    blank = jnp.zeros((ROWS, LANES), f32)
    pack_out[tiles * ROWS : (tiles + 1) * ROWS, :] = blank
    speed[tiles * ROWS : (tiles + 1) * ROWS, :] = blank

    def clear_slot(at, carry):
        slots[at] = tiles
        return carry

    def clear_count(at, carry):
        counts[at] = 0
        return carry

    def assign(block, carry):
        owner = owners[block]
        earlier = counts[owner]
        counts[owner] = earlier + 1
        slots[owner * capacity + earlier] = block
        return carry

    lax.fori_loop(0, group * capacity, clear_slot, 0)
    lax.fori_loop(0, group, clear_count, 0)
    lax.fori_loop(0, tiles, assign, 0)
    for at in range(group * capacity):
        block = slots[at]
        sent[at * 6 : at * 6 + 3, :] = tile_of(pack_out, block)[0:3, :]
        sent[at * 6 + 3 : at * 6 + 6, :] = tile_of(speed, block)[0:3, :]


def swap_neighbours(block, name):
    count = lax.axis_size(name)
    if count == 1:
        return block, block
    even = [(i, i ^ 1) for i in range(count)]
    first = lax.ppermute(block, name, even)
    if count == 2:
        return first, first
    odd = [(i, (i + 1) % count if i % 2 else (i - 1) % count) for i in range(count)]
    return first, lax.ppermute(block, name, odd)


def per_device(offsets, strength, ghost_list, pair_targets, pair_sources, owners):
    wide, tall, deep = (lax.axis_size(name) for name in everywhere)
    devices, group = wide * tall * deep, wide * tall
    segments = offsets.shape[1]
    tiles = segments // LANES
    ghost_tiles = ghost_list.shape[0] // LANES
    capacity = max(2, 2 * tiles // group)
    ghost_ids = ghost_list.reshape(ghost_tiles, LANES)
    in_vmem = pl.BlockSpec(memory_space=pltpu.VMEM)
    in_smem = pl.BlockSpec(memory_space=pltpu.SMEM)
    pack_type = jax.ShapeDtypeStruct((tiles * ROWS, LANES), f32)
    leaf_type = jax.ShapeDtypeStruct((devices * 4, LANES), f32)
    ghost_type = jax.ShapeDtypeStruct((ghost_tiles * ROWS, LANES), f32)
    work = pltpu.VMEM((TERMS * ROWS, LANES), f32)
    line = pltpu.VMEM((ROWS, LANES), f32)
    params = pltpu.CompilerParams(vmem_limit_bytes=48 << 20)

    pack, leaf, ghosts = pl.pallas_call(
        functools.partial(prologue_kernel, tiles, devices, deep),
        out_shape=(pack_type, leaf_type, ghost_type),
        in_specs=[in_vmem] * 3,
        out_specs=(in_vmem,) * 3,
        scratch_shapes=[work, line],
        compiler_params=params,
        name="prologue",
    )(offsets, strength, ghost_ids)
    table = pl.pallas_call(
        functools.partial(derivative_kernel, wide, tall, deep),
        out_shape=jax.ShapeDtypeStruct((TERMS, LANES), f32),
        out_specs=in_vmem,
        compiler_params=params,
        name="derivatives",
    )()
    beside = tuple((name, lax.axis_size(name)) for name in everywhere)
    places = tiles + 2 * len(beside) * ghost_tiles
    scratch = [
        pltpu.VMEM((places * FEATURES, LANES), bf16),
        pltpu.VMEM((tiles * FEATURES, LANES), bf16),
        pltpu.VMEM((places * 2 * ROWS, 2 * LANES), bf16),
        pltpu.VMEM((tiles * 2 * ROWS, LANES), f32),
        work,
        work,
        pltpu.VMEM((LANES, LANES), f32),
    ]
    taller = pltpu.VMEM(((tiles + 1) * ROWS, LANES), f32)
    for step_number in range(2):
        final = step_number == 1
        received = lax.all_to_all(leaf, everywhere, split_axis=0, concat_axis=0, tiled=True)
        arrived = []
        for name, count in beside:
            arrived.extend(swap_neighbours(ghosts, name))
        if final:
            out_shape = jax.ShapeDtypeStruct((group * capacity * 6, LANES), f32)
            out_specs = in_vmem
            extra = [taller, taller] + scratch + [
                pltpu.SMEM((group * capacity,), jnp.int32),
                pltpu.SMEM((group,), jnp.int32),
            ]
        else:
            out_shape = (pack_type, leaf_type, ghost_type)
            out_specs = (in_vmem,) * 3
            extra = [taller] + scratch + [line]
        result = pl.pallas_call(
            functools.partial(
                step_kernel, tiles, ghost_tiles, wide, tall, deep, beside, final, capacity
            ),
            out_shape=out_shape,
            in_specs=[in_smem] * 3 + [in_vmem] * (4 + len(arrived)),
            out_specs=out_specs,
            scratch_shapes=extra,
            compiler_params=params,
            name="last_step" if final else "step",
        )(pair_targets, pair_sources, owners[:, 0], pack, received, table, ghost_ids, *arrived)
        if not final:
            pack, leaf, ghosts = result
    handed = lax.all_to_all(result, ("gx", "gy"), split_axis=0, concat_axis=0, tiled=True)
    handed = handed.reshape(group * capacity, 6, LANES)
    return (handed[:, :3], handed[:, 3:])


def solution(mesh):
    return jax.shard_map(
        per_device,
        mesh=mesh,
        in_specs=(
            P(None, everywhere),
            P(None, everywhere),
            P(everywhere),
            P(everywhere),
            P(everywhere),
            P(everywhere, None),
        ),
        out_specs=(P(everywhere, None, None), P(everywhere, None, None)),
        check_vma=False,
    )
```

profile of v0, /device:TPU:0, one launch (start us, length us, event | category | flops | bytes accessed | tf_op | source)
XLA Modules:
  0.0 67.1 jit_solution(15294116801233120447)
XLA Ops:
  0.6 0.0 copy-start
  0.6 0.7 %copy-done = s32[1536]{0:T(1024)S(1)} copy-done((s32[1536]{0:T(1024)S(1)}, s32[1536]{0:T(1024)}, u32[]{:S(2)}) %copy-start) | copy-done | bytes 6168
  1.3 0.8 %copy-done.2 = f32[3,4096]{1,0:T(4,128)S(1)} copy-done((f32[3,4096]{1,0:T(4,128)S(1)}, f32[3,4096]{1,0:T(4,128)}, u32[]{:S(2)}) %copy-start.2) | copy-done | bytes 49176
  2.2 0.8 %copy-done.3 = f32[3,4096]{1,0:T(4,128)S(1)} copy-done((f32[3,4096]{1,0:T(4,128)S(1)}, f32[3,4096]{1,0:T(4,128)}, u32[]{:S(2)}) %copy-start.3) | copy-done | bytes 49176
  3.0 1.9 %prologue.1 = (f32[256,128]{1,0:T(8,128)S(1)}, f32[128,128]{1,0:T(8,128)}, f32[96,128]{1,0:T(8,128)S(1)}) custom-call(f32[3,4096]{1,0:T(4,128)S(1)} %copy-done.2, f32[3,4096]{1,0:T(4,128)S(1)} %copy-done.3, s32[12,128]{1,0:T(8,128)S(1)} %bitcast.10), custom_call_target="tpu_custom_call" | custom-call | tf_op jit(solution)/shard_map/prologue/pallas_call | solution.py:444
  4.9 7.3 %all-to-all-start = ((f32[32,4,128]{2,1,0:T(4,128)}), f32[32,4,128]{2,1,0:T(4,128)S(1)}, u32[]{:S(2)}, u32[]{:S(2)}) async-start(f32[32,4,128]{2,1,0:T(4,128)} %bitcast.2), calls=%async_computation | async-start | bytes 131072 | tf_op jit(solution)/shard_map/all_to_all | solution.py:474
  12.2 0.3 collective-permute-start.4
  12.6 2.5 %collective-permute-start.3 = (f32[96,128]{1,0:T(8,128)S(1)}, f32[96,128]{1,0:T(8,128)S(1)}, u32[]{:S(2)}, u32[]{:S(2)}) collective-permute-start(f32[96,128]{1,0:T(8,128)S(1)} %get-tuple-element.10), channel_id=1, source_target_pairs={{0,6},{2,4},{4,2},{6,0},{1,7},{3,5},{5,3},{7,1},{8,14},{10,12},{12... | collective-permute-start | bytes 147464 | tf_op jit(solution)/shard_map/ppermute | solution.py:424
  15.1 0.6 collective-permute-start.2
  15.7 3.4 %collective-permute-start.1 = (f32[96,128]{1,0:T(8,128)S(1)}, f32[96,128]{1,0:T(8,128)S(1)}, u32[]{:S(2)}, u32[]{:S(2)}) collective-permute-start(f32[96,128]{1,0:T(8,128)S(1)} %get-tuple-element.10), channel_id=1, source_target_pairs={{0,24},{8,16},{16,8},{24,0},{1,25},{9,17},{17,9},{25,1},{2,26},{10... | collective-permute-start | bytes 147464 | tf_op jit(solution)/shard_map/ppermute | solution.py:424
  19.0 0.0 collective-permute-start
  19.0 0.1 derivatives.1.table
  19.1 0.1 collective-permute-done.2.rest_2_
  19.2 2.4 %collective-permute-done.1.rest_1_ = f32[96,128]{1,0:T(8,128)S(1)} collective-permute-done((f32[96,128]{1,0:T(8,128)S(1)}, f32[96,128]{1,0:T(8,128)S(1)}, u32[]{:S(2)}, u32[]{:S(2)}) %collective-permute-start.1) | collective-permute-done | bytes 49184 | tf_op jit(solution)/shard_map/ppermute | solution.py:424
  21.6 1.5 %collective-permute-done.rest_0_ = f32[96,128]{1,0:T(8,128)S(1)} collective-permute-done((f32[96,128]{1,0:T(8,128)S(1)}, f32[96,128]{1,0:T(8,128)S(1)}, u32[]{:S(2)}, u32[]{:S(2)}) %collective-permute-start) | collective-permute-done | bytes 49184 | tf_op jit(solution)/shard_map/ppermute | solution.py:420
  23.1 0.6 copy-done.4
  23.8 0.0 copy-done.5
  23.8 0.0 copy-done.6
  23.8 8.4 %step.1 = (f32[256,128]{1,0:T(8,128)S(1)}, f32[128,128]{1,0:T(8,128)}, f32[96,128]{1,0:T(8,128)S(1)}) custom-call(s32[128]{0:T(128)S(1)} %copy-done.4, s32[128]{0:T(128)S(1)} %copy-done.5, s32[32]{0:T(128)S(1)} %bitcast.13, f32[256,128]{1,0:T(8,128)S(1)} %get-tuple-element.8.pack, f32[128,128]{1,0:T(8,128)S(1)} %bitcast.8, f32[56,128]{1,0:T(8,128)S(1)} %derivatives.1.table, ...), custom_call_target="tpu_custom_call" | custom-call | tf_op jit(solution)/shard_map/step/pallas_call | solution.py:489
  32.2 3.1 %all-to-all-start.1 = ((f32[32,4,128]{2,1,0:T(4,128)}), f32[32,4,128]{2,1,0:T(4,128)S(1)}, u32[]{:S(2)}, u32[]{:S(2)}) async-start(f32[32,4,128]{2,1,0:T(4,128)} %bitcast.4), calls=%async_computation.1 | async-start | bytes 131072 | tf_op jit(solution)/shard_map/all_to_all | solution.py:474
  35.3 0.3 collective-permute-start.9
  35.6 2.5 %collective-permute-start.8 = (f32[96,128]{1,0:T(8,128)S(1)}, f32[96,128]{1,0:T(8,128)S(1)}, u32[]{:S(2)}, u32[]{:S(2)}) collective-permute-start(f32[96,128]{1,0:T(8,128)S(1)} %get-tuple-element.13), channel_id=1, source_target_pairs={{0,6},{2,4},{4,2},{6,0},{1,7},{3,5},{5,3},{7,1},{8,14},{10,12},{12... | collective-permute-start | bytes 147464 | tf_op jit(solution)/shard_map/ppermute | solution.py:424
  38.2 0.6 collective-permute-start.7
  38.7 3.4 %collective-permute-start.6 = (f32[96,128]{1,0:T(8,128)S(1)}, f32[96,128]{1,0:T(8,128)S(1)}, u32[]{:S(2)}, u32[]{:S(2)}) collective-permute-start(f32[96,128]{1,0:T(8,128)S(1)} %get-tuple-element.13), channel_id=1, source_target_pairs={{0,24},{8,16},{16,8},{24,0},{1,25},{9,17},{17,9},{25,1},{2,26},{10... | collective-permute-start | bytes 147464 | tf_op jit(solution)/shard_map/ppermute | solution.py:424
  42.1 0.2 collective-permute-done.7.rest_2_
  42.3 2.4 %collective-permute-done.6.rest_1_ = f32[96,128]{1,0:T(8,128)S(1)} collective-permute-done((f32[96,128]{1,0:T(8,128)S(1)}, f32[96,128]{1,0:T(8,128)S(1)}, u32[]{:S(2)}, u32[]{:S(2)}) %collective-permute-start.6) | collective-permute-done | bytes 49184 | tf_op jit(solution)/shard_map/ppermute | solution.py:424
  44.6 1.5 %collective-permute-done.5.rest_0_ = f32[96,128]{1,0:T(8,128)S(1)} collective-permute-done((f32[96,128]{1,0:T(8,128)S(1)}, f32[96,128]{1,0:T(8,128)S(1)}, u32[]{:S(2)}, u32[]{:S(2)}) %collective-permute-start.5) | collective-permute-done | bytes 49184 | tf_op jit(solution)/shard_map/ppermute | solution.py:420
  46.2 7.5 %last_step.1 = f32[384,128]{1,0:T(8,128)S(1)} custom-call(s32[128]{0:T(128)S(1)} %copy-done.4, s32[128]{0:T(128)S(1)} %copy-done.5, s32[32]{0:T(128)S(1)} %bitcast.14, f32[256,128]{1,0:T(8,128)S(1)} %get-tuple-element.11.pack, f32[128,128]{1,0:T(8,128)S(1)} %bitcast.9, f32[56,128]{1,0:T(8,128)S(1)} %derivatives.1.table, s32[12,128]{1,0:T(8,128)S(1)} %bitcast.12, ...), custom_call_target="tpu_custom_call" | custom-call | tf_op jit(solution)/shard_map/last_step/pallas_call | solution.py:489
  53.7 12.0 %all_to_all.31 = f32[16,24,128]{2,1,0:T(8,128)S(1)} all-to-all(f32[16,24,128]{2,1,0:T(8,128)S(1)} %bitcast.7), channel_id=1, replica_groups=mesh['gx'=4,'gy'=4,'gz'=2] {'gx','gy'}, dimensions={0} | all-to-all | bytes 393216 | tf_op jit(solution)/shard_map/all_to_all | solution.py:502
  65.7 0.1 fusion
  65.8 0.6 copy.9
  66.4 0.6 copy.8
  (15 shorter events, 0.1 us)
Async XLA Ops:
  0.6 0.7 %copy-start = (s32[1536]{0:T(1024)S(1)}, s32[1536]{0:T(1024)}, u32[]{:S(2)}) copy-start(s32[1536]{0:T(1024)} %param.8) | copy-start | bytes 18436
  1.3 0.8 %copy-start.2 = (f32[3,4096]{1,0:T(4,128)S(1)}, f32[3,4096]{1,0:T(4,128)}, u32[]{:S(2)}) copy-start(f32[3,4096]{1,0:T(4,128)} %offsets.1) | copy-start | bytes 147460
  2.2 0.8 %copy-start.3 = (f32[3,4096]{1,0:T(4,128)S(1)}, f32[3,4096]{1,0:T(4,128)}, u32[]{:S(2)}) copy-start(f32[3,4096]{1,0:T(4,128)} %strength.1) | copy-start | bytes 147460
  4.9 18.2 %all-to-all-start = ((f32[32,4,128]{2,1,0:T(4,128)}), f32[32,4,128]{2,1,0:T(4,128)S(1)}, u32[]{:S(2)}, u32[]{:S(2)}) async-start(f32[32,4,128]{2,1,0:T(4,128)} %bitcast.2), calls=%async_computation | async-start | bytes 131072 | tf_op jit(solution)/shard_map/all_to_all | solution.py:474
  12.2 6.9 %collective-permute-start.4 = (f32[96,128]{1,0:T(8,128)S(1)}, f32[96,128]{1,0:T(8,128)S(1)}, u32[]{:S(2)}, u32[]{:S(2)}) collective-permute-start(f32[96,128]{1,0:T(8,128)S(1)} %get-tuple-element.10), channel_id=1, source_target_pairs={{0,1},{1,0},{2,3},{3,2},{4,5},{5,4},{6,7},{7,6},{8,9},{9,8},{10,11... | collective-permute-start | bytes 147464 | tf_op jit(solution)/shard_map/ppermute | solution.py:420
  12.6 6.6 %collective-permute-start.3 = (f32[96,128]{1,0:T(8,128)S(1)}, f32[96,128]{1,0:T(8,128)S(1)}, u32[]{:S(2)}, u32[]{:S(2)}) collective-permute-start(f32[96,128]{1,0:T(8,128)S(1)} %get-tuple-element.10), channel_id=1, source_target_pairs={{0,6},{2,4},{4,2},{6,0},{1,7},{3,5},{5,3},{7,1},{8,14},{10,12},{12... | collective-permute-start | bytes 147464 | tf_op jit(solution)/shard_map/ppermute | solution.py:424
  15.1 4.1 %collective-permute-start.2 = (f32[96,128]{1,0:T(8,128)S(1)}, f32[96,128]{1,0:T(8,128)S(1)}, u32[]{:S(2)}, u32[]{:S(2)}) collective-permute-start(f32[96,128]{1,0:T(8,128)S(1)} %get-tuple-element.10), channel_id=1, source_target_pairs={{0,2},{2,0},{4,6},{6,4},{1,3},{3,1},{5,7},{7,5},{8,10},{10,8},{12,... | collective-permute-start | bytes 147464 | tf_op jit(solution)/shard_map/ppermute | solution.py:420
  15.7 5.9 %collective-permute-start.1 = (f32[96,128]{1,0:T(8,128)S(1)}, f32[96,128]{1,0:T(8,128)S(1)}, u32[]{:S(2)}, u32[]{:S(2)}) collective-permute-start(f32[96,128]{1,0:T(8,128)S(1)} %get-tuple-element.10), channel_id=1, source_target_pairs={{0,24},{8,16},{16,8},{24,0},{1,25},{9,17},{17,9},{25,1},{2,26},{10... | collective-permute-start | bytes 147464 | tf_op jit(solution)/shard_map/ppermute | solution.py:424
  19.0 4.1 %collective-permute-start = (f32[96,128]{1,0:T(8,128)S(1)}, f32[96,128]{1,0:T(8,128)S(1)}, u32[]{:S(2)}, u32[]{:S(2)}) collective-permute-start(f32[96,128]{1,0:T(8,128)S(1)} %get-tuple-element.10), channel_id=1, source_target_pairs={{0,8},{8,0},{16,24},{24,16},{1,9},{9,1},{17,25},{25,17},{2,10},{10... | collective-permute-start | bytes 147464 | tf_op jit(solution)/shard_map/ppermute | solution.py:420
  19.0 4.1 %copy-start.1 = (s32[1536]{0:T(1024)S(1)}, s32[1536]{0:T(1024)}, u32[]{:S(2)}) copy-start(s32[1536]{0:T(1024)} %param.8) | copy-start | bytes 18436
  23.1 0.7 copy-start.4
  23.1 0.7 copy-start.5
  23.1 0.7 %copy-start.6 = (s32[32,1]{0,1:T(1,128)S(1)}, s32[32,1]{0,1:T(1,128)}, u32[]{:S(2)}) copy-start(s32[32,1]{0,1:T(1,128)} %param.11) | copy-start | bytes 388
  32.2 14.0 %all-to-all-start.1 = ((f32[32,4,128]{2,1,0:T(4,128)}), f32[32,4,128]{2,1,0:T(4,128)S(1)}, u32[]{:S(2)}, u32[]{:S(2)}) async-start(f32[32,4,128]{2,1,0:T(4,128)} %bitcast.4), calls=%async_computation.1 | async-start | bytes 131072 | tf_op jit(solution)/shard_map/all_to_all | solution.py:474
  35.3 6.8 %collective-permute-start.9 = (f32[96,128]{1,0:T(8,128)S(1)}, f32[96,128]{1,0:T(8,128)S(1)}, u32[]{:S(2)}, u32[]{:S(2)}) collective-permute-start(f32[96,128]{1,0:T(8,128)S(1)} %get-tuple-element.13), channel_id=1, source_target_pairs={{0,1},{1,0},{2,3},{3,2},{4,5},{5,4},{6,7},{7,6},{8,9},{9,8},{10,11... | collective-permute-start | bytes 147464 | tf_op jit(solution)/shard_map/ppermute | solution.py:420
  35.6 6.5 %collective-permute-start.8 = (f32[96,128]{1,0:T(8,128)S(1)}, f32[96,128]{1,0:T(8,128)S(1)}, u32[]{:S(2)}, u32[]{:S(2)}) collective-permute-start(f32[96,128]{1,0:T(8,128)S(1)} %get-tuple-element.13), channel_id=1, source_target_pairs={{0,6},{2,4},{4,2},{6,0},{1,7},{3,5},{5,3},{7,1},{8,14},{10,12},{12... | collective-permute-start | bytes 147464 | tf_op jit(solution)/shard_map/ppermute | solution.py:424
  38.2 4.1 %collective-permute-start.7 = (f32[96,128]{1,0:T(8,128)S(1)}, f32[96,128]{1,0:T(8,128)S(1)}, u32[]{:S(2)}, u32[]{:S(2)}) collective-permute-start(f32[96,128]{1,0:T(8,128)S(1)} %get-tuple-element.13), channel_id=1, source_target_pairs={{0,2},{2,0},{4,6},{6,4},{1,3},{3,1},{5,7},{7,5},{8,10},{10,8},{12,... | collective-permute-start | bytes 147464 | tf_op jit(solution)/shard_map/ppermute | solution.py:420
  38.7 5.9 %collective-permute-start.6 = (f32[96,128]{1,0:T(8,128)S(1)}, f32[96,128]{1,0:T(8,128)S(1)}, u32[]{:S(2)}, u32[]{:S(2)}) collective-permute-start(f32[96,128]{1,0:T(8,128)S(1)} %get-tuple-element.13), channel_id=1, source_target_pairs={{0,24},{8,16},{16,8},{24,0},{1,25},{9,17},{17,9},{25,1},{2,26},{10... | collective-permute-start | bytes 147464 | tf_op jit(solution)/shard_map/ppermute | solution.py:424
  42.1 4.1 %collective-permute-start.5 = (f32[96,128]{1,0:T(8,128)S(1)}, f32[96,128]{1,0:T(8,128)S(1)}, u32[]{:S(2)}, u32[]{:S(2)}) collective-permute-start(f32[96,128]{1,0:T(8,128)S(1)} %get-tuple-element.13), channel_id=1, source_target_pairs={{0,8},{8,0},{16,24},{24,16},{1,9},{9,1},{17,25},{25,17},{2,10},{10... | collective-permute-start | bytes 147464 | tf_op jit(solution)/shard_map/ppermute | solution.py:420
where the time goes:
time: 67.4 us; the launch traced here: 67.1 us
  starting transfers between devices  23.9 us (35%)
  Pallas kernels  17.9 us (27%)
  blocking collectives  12 us (18%)
  waiting for transfers between devices  8.06 us (12%)
  local copies, waits for them, and re-layouts  4.42 us (7%)
  between operations  0.73 us (1%)
    pallas_call x2, Pallas kernels, per_device(): pl.pallas_call(functools.partial(step_kernel, tiles, ghost_tiles, wide, t...  15.9 us
    all_to_all x1, blocking collectives, per_device(): lax.all_to_all(result, ('gx', 'gy'), split_axis=0, concat_axis=0, tiled=T...  12 us
    ppermute x4, starting transfers between devices, swap_neighbours(): return (first, lax.ppermute(block, name, odd))  11.8 us
    all_to_all x2, starting transfers between devices, per_device(): lax.all_to_all(leaf, everywhere, split_axis=0, concat_axis=0, tiled=True)  10.4 us
    ppermute x4, waiting for transfers between devices, swap_neighbours(): return (first, lax.ppermute(block, name, odd))  4.71 us
    unnamed x16, local copies, waits for them, and re-layouts  4.34 us
    ppermute x6, waiting for transfers between devices, swap_neighbours(): first = lax.ppermute(block, name, even)  3.34 us
    pallas_call x1, Pallas kernels, per_device(): pl.pallas_call(functools.partial(prologue_kernel, tiles, devices, deep),...  1.9 us
  transfers between devices with their start and end apart: 12, of which 6 were waited for; matrix products, arithmetic and copies ran while one was open for 0% of the time, Pallas kernels for 0%

commit v1 on v0

--- a/solution.py
+++ b/solution.py
@@ -9,6 +9,7 @@
 from jax.experimental.pallas import tpu as pltpu
 from jax.sharding import PartitionSpec as P
 
+
 ORDER = 5
 LANES = 128
 ROWS = 8
@@ -66,7 +67,7 @@
     ]
 
 
-def leaf_moments(pack, tiles, devices, leaf, work, line):
+def moments_kernel(tiles, devices, pack, leaf, work, line):
     middle_x, middle_y, _ = slab_middle(1)
     middle = (middle_x, middle_y, 0.5)
     low = row_ids() < 4
@@ -99,7 +100,7 @@
             for c in range(ORDER + 1 - a - b)
         ]
         zero = jnp.zeros((ROWS, LANES), f32)
-        sums = lax.fori_loop(0, tiles // 2, body, tuple(zero for _ in names))
+        sums = lax.fori_loop(0, tiles // 2, body, tuple(zero for _ in names), unroll=4)
         for name, total in zip(names, sums):
             spot = PLACE[name]
             factor = (-1.0) ** sum(name) / FACTORIAL[spot]
@@ -131,7 +132,15 @@
         ghosts[out_tile * ROWS : (out_tile + 1) * ROWS, :] = found
 
 
-def prologue_kernel(tiles, devices, deep, offsets, strength, ghost_ids, pack, leaf, ghosts, work, line):
+def prologue_kernel(tiles, deep, offsets_in, strength_in, ids_in, pack, ghosts, offsets, strength, ghost_ids, arrivals):
+    loads = [
+        pltpu.make_async_copy(source, target, arrivals.at[number])
+        for number, (source, target) in enumerate(
+            ((offsets_in, offsets), (strength_in, strength), (ids_in, ghost_ids))
+        )
+    ]
+    for load in loads:
+        load.start()
     side_z = 1.0 / deep
     axis = lax.broadcasted_iota(jnp.int32, (3, LANES), 0)
     corner = jnp.where(
@@ -143,6 +152,8 @@
     )
     sides = jnp.where(axis == 2, side_z, 1.0)
     blank = jnp.zeros((1, LANES), f32)
+    for load in loads:
+        load.wait()
     for tile in range(tiles):
         span = slice(tile * LANES, (tile + 1) * LANES)
         base = tile * ROWS
@@ -150,7 +161,6 @@
         pack[base + 3 : base + 4, :] = blank
         pack[base + 4 : base + 7, :] = strength[:, span]
         pack[base + 7 : base + 8, :] = blank
-    leaf_moments(pack, tiles, devices, leaf, work, line)
     pick_ghosts(pack, tiles, ghost_ids, ghosts)
 
 
@@ -249,61 +259,11 @@
     store_features(place, targets, [join(one, two), join(one, two), join(three, one), sizes])
 
 
-def step_kernel(
-    tiles, ghost_tiles, wide, tall, deep, beside, final, capacity,
-    pair_targets, pair_sources, owners, pack, received, table, ghost_ids, *rest,
-):
-    devices = wide * tall * deep
-    columns = wide * tall
+def near_kernel(tiles, ghost_tiles, deep, beside, pair_targets, pair_sources, pack, *rest):
     ghost_in = rest[: 2 * len(beside)]
-    rest = rest[2 * len(beside) :]
-    if final:
-        sent, pack_out, speed, sources, targets, pushes, near, work, expansion, square, slots, counts = rest
-    else:
-        pack_out, leaf, ghosts, speed, sources, targets, pushes, near, work, expansion, square, line = rest
+    close, sources, targets, pushes, near = rest[2 * len(beside) :]
     row = row_ids()
     middle = slab_middle(deep)
-
-    square[...] = jnp.zeros_like(square)
-    work[...] = jnp.zeros_like(work)
-    for k in range(3):
-        total = received[pl.ds(k, columns, stride=4 * deep), :]
-        for slab in range(1, deep):
-            total = total + received[pl.ds(slab * 4 + k, columns, stride=4 * deep), :]
-        square[0:columns, :] = total
-        turned = square[...].T[0:TERMS, :]
-        work[pl.ds(k, TERMS, stride=ROWS), :] = turned
-        work[pl.ds(k + 4, TERMS, stride=ROWS), :] = turned
-    for spot, outer in enumerate(POWERS):
-        total = None
-        for inner_spot, inner in enumerate(POWERS):
-            if sum(outer) + sum(inner) > ORDER:
-                continue
-            merged = tuple(o + i for o, i in zip(outer, inner))
-            term = spread(table, PLACE[merged]) * work[inner_spot * ROWS : (inner_spot + 1) * ROWS, :]
-            total = term if total is None else total + term
-        summed = jnp.sum(total, axis=1, keepdims=True) * (1.0 / FACTORIAL[spot])
-        expansion[spot * ROWS : (spot + 1) * ROWS, :] = jnp.broadcast_to(summed, (ROWS, LANES))
-
-    def evaluate(pair, carry):
-        x, y, z = relative_pair(pack, pair, middle)
-        over_x = None
-        for a in range(ORDER, -1, -1):
-            over_y = None
-            for b in range(ORDER - a, -1, -1):
-                over_z = None
-                for c in range(ORDER - a - b, -1, -1):
-                    spot = PLACE[a, b, c]
-                    factor = expansion[spot * ROWS : (spot + 1) * ROWS, :]
-                    over_z = factor if over_z is None else over_z * z + factor
-                over_y = over_z if over_y is None else over_y * y + over_z
-            over_x = over_y if over_x is None else over_x * x + over_y
-        spot = pl.multiple_of(pair * (2 * ROWS), 2 * ROWS)
-        speed[pl.ds(spot, ROWS), :] = over_x
-        speed[pl.ds(spot + ROWS, ROWS), :] = pltpu.roll(over_x, 4, 0)
-        return carry
-
-    lax.fori_loop(0, tiles // 2, evaluate, 0)
 
     def own_tile(tile, carry):
         value = tile_of(pack, tile)
@@ -366,12 +326,70 @@
 
     lax.fori_loop(0, pair_count // batch, batch_of_pairs, 0)
 
-    def advance(tile, carry):
+    def collect(tile, carry):
         spot = pl.multiple_of(tile * 2 * ROWS, 2 * ROWS)
         upper, lower = near[pl.ds(spot, ROWS), :], near[pl.ds(spot + ROWS, ROWS), :]
-        close = upper + pltpu.roll(upper, 4, 0) + lower
-        velocity = jnp.where(row < 3, close + tile_of(speed, tile), 0.0)
+        close[pl.ds(pl.multiple_of(tile * ROWS, ROWS), ROWS), :] = upper + pltpu.roll(upper, 4, 0) + lower
+        return carry
+
+    lax.fori_loop(0, tiles, collect, 0, unroll=4)
+
+
+def far_kernel(tiles, wide, tall, deep, final, capacity, chosen, pack, close, received, table, *rest):
+    columns = wide * tall
+    if final:
+        owners = chosen
+        sent, pack_out, speed, work, expansion, square, slots, counts = rest
+    else:
+        ghost_ids = chosen
+        pack_out, ghosts, speed, work, expansion, square = rest
+    row = row_ids()
+    middle = slab_middle(deep)
+
+    square[...] = jnp.zeros_like(square)
+    work[...] = jnp.zeros_like(work)
+    for k in range(3):
+        total = received[pl.ds(k, columns, stride=4 * deep), :]
+        for slab in range(1, deep):
+            total = total + received[pl.ds(slab * 4 + k, columns, stride=4 * deep), :]
+        square[0:columns, :] = total
+        turned = square[...].T[0:TERMS, :]
+        work[pl.ds(k, TERMS, stride=ROWS), :] = turned
+        work[pl.ds(k + 4, TERMS, stride=ROWS), :] = turned
+    for spot, outer in enumerate(POWERS):
+        total = None
+        for inner_spot, inner in enumerate(POWERS):
+            if sum(outer) + sum(inner) > ORDER:
+                continue
+            merged = tuple(o + i for o, i in zip(outer, inner))
+            term = spread(table, PLACE[merged]) * work[inner_spot * ROWS : (inner_spot + 1) * ROWS, :]
+            total = term if total is None else total + term
+        summed = jnp.sum(total, axis=1, keepdims=True) * (1.0 / FACTORIAL[spot])
+        expansion[spot * ROWS : (spot + 1) * ROWS, :] = jnp.broadcast_to(summed, (ROWS, LANES))
+
+    def evaluate(pair, carry):
+        x, y, z = relative_pair(pack, pair, middle)
+        over_x = None
+        for a in range(ORDER, -1, -1):
+            over_y = None
+            for b in range(ORDER - a, -1, -1):
+                over_z = None
+                for c in range(ORDER - a - b, -1, -1):
+                    spot = PLACE[a, b, c]
+                    factor = expansion[spot * ROWS : (spot + 1) * ROWS, :]
+                    over_z = factor if over_z is None else over_z * z + factor
+                over_y = over_z if over_y is None else over_y * y + over_z
+            over_x = over_y if over_x is None else over_x * x + over_y
+        spot = pl.multiple_of(pair * (2 * ROWS), 2 * ROWS)
+        speed[pl.ds(spot, ROWS), :] = over_x
+        speed[pl.ds(spot + ROWS, ROWS), :] = pltpu.roll(over_x, 4, 0)
+        return carry
+
+    lax.fori_loop(0, tiles // 2, evaluate, 0, unroll=4)
+
+    def advance(tile, carry):
         place = pl.ds(pl.multiple_of(tile * ROWS, ROWS), ROWS)
+        velocity = jnp.where(row < 3, close[place, :] + speed[place, :], 0.0)
         speed[place, :] = velocity
         pack_out[place, :] = pack[place, :] + time_step * velocity
         return carry
@@ -379,7 +397,6 @@
     lax.fori_loop(0, tiles, advance, 0, unroll=4)
 
     if not final:
-        leaf_moments(pack_out, tiles, devices, leaf, work, line)
         pick_ghosts(pack_out, tiles, ghost_ids, ghosts)
         return
 
@@ -410,6 +427,13 @@
         block = slots[at]
         sent[at * 6 : at * 6 + 3, :] = tile_of(pack_out, block)[0:3, :]
         sent[at * 6 + 3 : at * 6 + 6, :] = tile_of(speed, block)[0:3, :]
+
+
+def receive_kernel(handed, positions, velocity):
+    count = positions.shape[1]
+    for axis in range(3):
+        positions[axis] = handed[pl.ds(axis, count, stride=6), :]
+        velocity[axis] = handed[pl.ds(axis + 3, count, stride=6), :]
 
 
 def swap_neighbours(block, name):
@@ -420,6 +444,15 @@
     first = lax.ppermute(block, name, even)
     if count == 2:
         return first, first
+    deep = lax.axis_size("gz")
+    if name != "gz" and deep % 2 == 0:
+        odd = []
+        for i in range(count):
+            for k in range(deep):
+                end = i in (0, count - 1)
+                other = i * deep + (k ^ 1) if end else (i + 1 if i % 2 else i - 1) * deep + k
+                odd.append((i * deep + k, other))
+        return first, lax.ppermute(block, (name, "gz"), odd)
     odd = [(i, (i + 1) % count if i % 2 else (i - 1) % count) for i in range(count)]
     return first, lax.ppermute(block, name, odd)
 
@@ -441,15 +474,22 @@
     line = pltpu.VMEM((ROWS, LANES), f32)
     params = pltpu.CompilerParams(vmem_limit_bytes=48 << 20)
 
-    pack, leaf, ghosts = pl.pallas_call(
-        functools.partial(prologue_kernel, tiles, devices, deep),
-        out_shape=(pack_type, leaf_type, ghost_type),
-        in_specs=[in_vmem] * 3,
-        out_specs=(in_vmem,) * 3,
-        scratch_shapes=[work, line],
+    in_place = pl.BlockSpec(memory_space=pltpu.HBM)
+
+    pack, ghosts = pl.pallas_call(
+        functools.partial(prologue_kernel, tiles, deep),
+        out_shape=(pack_type, ghost_type),
+        in_specs=[in_place] * 3,
+        out_specs=(in_vmem,) * 2,
+        scratch_shapes=[
+            pltpu.VMEM(offsets.shape, f32),
+            pltpu.VMEM(strength.shape, f32),
+            pltpu.VMEM(ghost_ids.shape, jnp.int32),
+            pltpu.SemaphoreType.DMA((3,)),
+        ],
         compiler_params=params,
         name="prologue",
-    )(offsets, strength, ghost_ids)
+    )(*(pltpu.with_memory_space_constraint(value, pltpu.HBM) for value in (offsets, strength, ghost_ids)))
     table = pl.pallas_call(
         functools.partial(derivative_kernel, wide, tall, deep),
         out_shape=jax.ShapeDtypeStruct((TERMS, LANES), f32),
@@ -459,49 +499,70 @@
     )()
     beside = tuple((name, lax.axis_size(name)) for name in everywhere)
     places = tiles + 2 * len(beside) * ghost_tiles
-    scratch = [
-        pltpu.VMEM((places * FEATURES, LANES), bf16),
-        pltpu.VMEM((tiles * FEATURES, LANES), bf16),
-        pltpu.VMEM((places * 2 * ROWS, 2 * LANES), bf16),
-        pltpu.VMEM((tiles * 2 * ROWS, LANES), f32),
-        work,
-        work,
-        pltpu.VMEM((LANES, LANES), f32),
-    ]
     taller = pltpu.VMEM(((tiles + 1) * ROWS, LANES), f32)
     for step_number in range(2):
         final = step_number == 1
-        received = lax.all_to_all(leaf, everywhere, split_axis=0, concat_axis=0, tiled=True)
         arrived = []
         for name, count in beside:
             arrived.extend(swap_neighbours(ghosts, name))
+        leaf = pl.pallas_call(
+            functools.partial(moments_kernel, tiles, devices),
+            out_shape=leaf_type,
+            in_specs=[in_vmem],
+            out_specs=in_vmem,
+            scratch_shapes=[work, line],
+            compiler_params=params,
+            name="moments",
+        )
+        leaf = leaf(pack)
+        received = lax.all_to_all(leaf, everywhere, split_axis=0, concat_axis=0, tiled=True)
+        close = pl.pallas_call(
+            functools.partial(near_kernel, tiles, ghost_tiles, deep, beside),
+            out_shape=pack_type,
+            in_specs=[in_smem] * 2 + [in_vmem] * (1 + len(arrived)),
+            out_specs=in_vmem,
+            scratch_shapes=[
+                pltpu.VMEM((places * FEATURES, LANES), bf16),
+                pltpu.VMEM((tiles * FEATURES, LANES), bf16),
+                pltpu.VMEM((places * 2 * ROWS, 2 * LANES), bf16),
+                pltpu.VMEM((tiles * 2 * ROWS, LANES), f32),
+            ],
+            compiler_params=params,
+            name="near",
+        )(pair_targets, pair_sources, pack, *arrived)
         if final:
             out_shape = jax.ShapeDtypeStruct((group * capacity * 6, LANES), f32)
             out_specs = in_vmem
-            extra = [taller, taller] + scratch + [
+            extra = [taller, taller, work, work, pltpu.VMEM((LANES, LANES), f32)] + [
                 pltpu.SMEM((group * capacity,), jnp.int32),
                 pltpu.SMEM((group,), jnp.int32),
             ]
         else:
-            out_shape = (pack_type, leaf_type, ghost_type)
-            out_specs = (in_vmem,) * 3
-            extra = [taller] + scratch + [line]
+            out_shape = (pack_type, ghost_type)
+            out_specs = (in_vmem,) * 2
+            extra = [taller, work, work, pltpu.VMEM((LANES, LANES), f32)]
         result = pl.pallas_call(
-            functools.partial(
-                step_kernel, tiles, ghost_tiles, wide, tall, deep, beside, final, capacity
-            ),
+            functools.partial(far_kernel, tiles, wide, tall, deep, final, capacity),
             out_shape=out_shape,
-            in_specs=[in_smem] * 3 + [in_vmem] * (4 + len(arrived)),
+            in_specs=[in_smem if final else in_vmem] + [in_vmem] * 4,
             out_specs=out_specs,
             scratch_shapes=extra,
             compiler_params=params,
-            name="last_step" if final else "step",
-        )(pair_targets, pair_sources, owners[:, 0], pack, received, table, ghost_ids, *arrived)
+            name="last_far" if final else "far",
+        )(owners[:, 0] if final else ghost_ids, pack, close, received, table)
         if not final:
-            pack, leaf, ghosts = result
+            pack, ghosts = result
     handed = lax.all_to_all(result, ("gx", "gy"), split_axis=0, concat_axis=0, tiled=True)
-    handed = handed.reshape(group * capacity, 6, LANES)
-    return (handed[:, :3], handed[:, 3:])
+    moved = jax.ShapeDtypeStruct((3, group * capacity, LANES), f32)
+    moved = pl.pallas_call(
+        receive_kernel,
+        out_shape=(moved, moved),
+        in_specs=[in_vmem],
+        out_specs=(in_vmem,) * 2,
+        compiler_params=params,
+        name="receive",
+    )(handed)
+    return tuple(value.transpose(1, 0, 2) for value in moved)
 
 
 def solution(mesh):

time: 67.4 us -> 62.1 us (0.921)
  waiting for transfers between devices: 8.06 us -> 4.01 us
  local copies, waits for them, and re-layouts: 4.42 us -> 0.67 us
  Pallas kernels: 17.9 us -> 19.5 us
  blocking collectives: 12 us -> 13.1 us
    ppermute x4, starting transfers between devices: 11.8 us -> 0.52 us  [swap_neighbours(): return (first, lax.ppermute(block, (name, 'gz'), odd))]
    ppermute x6, starting transfers between devices: 1.76 us -> 12.2 us  [swap_neighbours(): first = lax.ppermute(block, name, even)]
    ppermute x4, waiting for transfers between devices: 4.71 us -> 0.01 us  [swap_neighbours(): return (first, lax.ppermute(block, (name, 'gz'), odd))]
    unnamed x16 -> x8, local copies, waits for them, and re-layouts: 4.34 us -> 0.67 us
    pallas_call x3 -> x8, Pallas kernels: 17.8 us -> 19.4 us  [the longest x2 11.5 us: per_device(): pl.pallas_call(functools.partial(near_kernel, tiles, ghost_tiles, deep, b...]
    all_to_all x1, blocking collectives: 12 us -> 13.1 us  [per_device(): lax.all_to_all(result, ('gx', 'gy'), split_axis=0, concat_axis=0, tiled=T...]
  transfers between devices with their start and end apart: 12 -> 12, of which waited for: 6 -> 4; matrix products, arithmetic and copies ran while one was open for 0% -> 0% of each run, Pallas kernels for 0% -> 19%
where the time goes in v1:
time: 62.1 us; the launch traced here: 61.8 us
  starting transfers between devices  23.8 us (38%)
  Pallas kernels  19.5 us (31%)
  blocking collectives  13.1 us (21%)
  waiting for transfers between devices  4.01 us (6%)
  between operations  0.78 us (1%)
  local copies, waits for them, and re-layouts  0.67 us (1%)
    all_to_all x1, blocking collectives, per_device(): lax.all_to_all(result, ('gx', 'gy'), split_axis=0, concat_axis=0, tiled=T...  13.1 us
    ppermute x6, starting transfers between devices, swap_neighbours(): first = lax.ppermute(block, name, even)  12.2 us
    pallas_call x2, Pallas kernels, per_device(): pl.pallas_call(functools.partial(near_kernel, tiles, ghost_tiles, deep, b...  11.5 us
    all_to_all x2, starting transfers between devices, per_device(): lax.all_to_all(leaf, everywhere, split_axis=0, concat_axis=0, tiled=True)  11.1 us
    ppermute x6, waiting for transfers between devices, swap_neighbours(): first = lax.ppermute(block, name, even)  4 us
    pallas_call x2, Pallas kernels, per_device(): pl.pallas_call(functools.partial(far_kernel, tiles, wide, tall, deep, fin...  3.37 us
    pallas_call x2, Pallas kernels, per_device(): leaf = leaf(pack)  2.36 us
    pallas_call x1, Pallas kernels, per_device(): pl.pallas_call(functools.partial(prologue_kernel, tiles, deep), out_shape...  1.43 us
  transfers between devices with their start and end apart: 12, of which 4 were waited for; matrix products, arithmetic and copies ran while one was open for 0% of the time, Pallas kernels for 19%

profile of v1, /device:TPU:0, one launch (start us, length us, event | category | flops | bytes accessed | tf_op | source)
XLA Modules:
  0.0 61.8 jit_solution(12810039522200768021)
XLA Ops:
  0.6 1.4 %prologue.1 = (f32[256,128]{1,0:T(8,128)S(1)}, f32[96,128]{1,0:T(8,128)S(1)}) custom-call(f32[3,4096]{1,0:T(4,128)} %offsets_in.1, f32[3,4096]{1,0:T(4,128)} %strength_in.1, s32[12,128]{1,0:T(8,128)} %bitcast.14), custom_call_target="tpu_custom_call" | custom-call | tf_op jit(solution)/shard_map/prologue/pallas_call | solution.py:479
  2.1 1.2 %moments.2 = f32[128,128]{1,0:T(8,128)} custom-call(f32[256,128]{1,0:T(8,128)S(1)} %get-tuple-element.8.pack), custom_call_target="tpu_custom_call" | custom-call | tf_op jit(solution)/shard_map/moments/pallas_call | solution.py:517
  3.3 7.3 %all-to-all-start = ((f32[32,4,128]{2,1,0:T(4,128)}), f32[32,4,128]{2,1,0:T(4,128)S(1)}, u32[]{:S(2)}, u32[]{:S(2)}) async-start(f32[32,4,128]{2,1,0:T(4,128)} %bitcast.2), calls=%async_computation | async-start | bytes 131072 | tf_op jit(solution)/shard_map/all_to_all | solution.py:518
  10.6 0.0 copy-start.1
  10.6 0.0 copy-start.2
  10.6 0.3 collective-permute-start.4
  10.9 0.3 collective-permute-start.3
  11.2 2.8 %collective-permute-start.2 = (f32[96,128]{1,0:T(8,128)S(1)}, f32[96,128]{1,0:T(8,128)S(1)}, u32[]{:S(2)}, u32[]{:S(2)}) collective-permute-start(f32[96,128]{1,0:T(8,128)S(1)} %get-tuple-element.9), channel_id=1, source_target_pairs={{0,2},{2,0},{4,6},{6,4},{1,3},{3,1},{5,7},{7,5},{8,10},{10,8},{12,... | collective-permute-start | bytes 147464 | tf_op jit(solution)/shard_map/ppermute | solution.py:444
  14.0 0.0 collective-permute-start.1
  14.0 3.0 %collective-permute-start = (f32[96,128]{1,0:T(8,128)S(1)}, f32[96,128]{1,0:T(8,128)S(1)}, u32[]{:S(2)}, u32[]{:S(2)}) collective-permute-start(f32[96,128]{1,0:T(8,128)S(1)} %get-tuple-element.9), channel_id=1, source_target_pairs={{0,8},{8,0},{16,24},{24,16},{1,9},{9,1},{17,25},{25,17},{2,10},{10... | collective-permute-start | bytes 147464 | tf_op jit(solution)/shard_map/ppermute | solution.py:444
  17.0 0.1 derivatives.1.table
  17.1 0.0 copy-start
  17.1 0.0 collective-permute-done.3.rest_3_
  17.1 0.4 collective-permute-done.2.rest_2_
  17.5 0.0 collective-permute-done.1.rest_1_
  17.5 1.6 %collective-permute-done.rest_0_ = f32[96,128]{1,0:T(8,128)S(1)} collective-permute-done((f32[96,128]{1,0:T(8,128)S(1)}, f32[96,128]{1,0:T(8,128)S(1)}, u32[]{:S(2)}, u32[]{:S(2)}) %collective-permute-start) | collective-permute-done | bytes 49184 | tf_op jit(solution)/shard_map/ppermute | solution.py:444
  19.0 5.8 %near.2.close = f32[256,128]{1,0:T(8,128)S(1)} custom-call(s32[128]{0:T(128)S(1)} %copy-done.1, s32[128]{0:T(128)S(1)} %copy-done.2, f32[256,128]{1,0:T(8,128)S(1)} %get-tuple-element.8.pack, f32[96,128]{1,0:T(8,128)S(1)} %collective-permute-done.rest_0_, f32[96,128]{1,0:T(8,128)S(1)} %collective-permute-done.1.rest_1_, ...), custom_call_target="tpu_custom_call" | custom-call | tf_op jit(solution)/shard_map/near/pallas_call | solution.py:519
  24.8 1.2 %far.1 = (f32[256,128]{1,0:T(8,128)S(1)}, f32[96,128]{1,0:T(8,128)S(1)}) custom-call(s32[12,128]{1,0:T(8,128)S(1)} %bitcast.15, f32[256,128]{1,0:T(8,128)S(1)} %get-tuple-element.8.pack, f32[256,128]{1,0:T(8,128)S(1)} %near.2.close, f32[128,128]{1,0:T(8,128)S(1)} %bitcast.13, f32[56,128]{1,0:T(8,128)S(1)} %derivatives.1.table), custom_call_target="tpu_custom_call" | custom-call | tf_op jit(solution)/shard_map/far/pallas_call | solution.py:544
  26.0 1.2 %moments.3 = f32[128,128]{1,0:T(8,128)} custom-call(f32[256,128]{1,0:T(8,128)S(1)} %get-tuple-element.10.pack), custom_call_target="tpu_custom_call" | custom-call | tf_op jit(solution)/shard_map/moments/pallas_call | solution.py:517
  27.2 3.7 %all-to-all-start.1 = ((f32[32,4,128]{2,1,0:T(4,128)}), f32[32,4,128]{2,1,0:T(4,128)S(1)}, u32[]{:S(2)}, u32[]{:S(2)}) async-start(f32[32,4,128]{2,1,0:T(4,128)} %bitcast.4), calls=%async_computation.1 | async-start | bytes 131072 | tf_op jit(solution)/shard_map/all_to_all | solution.py:518
  30.9 0.3 collective-permute-start.9
  31.3 0.3 collective-permute-start.8
  31.5 2.8 %collective-permute-start.7 = (f32[96,128]{1,0:T(8,128)S(1)}, f32[96,128]{1,0:T(8,128)S(1)}, u32[]{:S(2)}, u32[]{:S(2)}) collective-permute-start(f32[96,128]{1,0:T(8,128)S(1)} %get-tuple-element.11), channel_id=1, source_target_pairs={{0,2},{2,0},{4,6},{6,4},{1,3},{3,1},{5,7},{7,5},{8,10},{10,8},{12,... | collective-permute-start | bytes 147464 | tf_op jit(solution)/shard_map/ppermute | solution.py:444
  34.4 3.0 %collective-permute-start.5 = (f32[96,128]{1,0:T(8,128)S(1)}, f32[96,128]{1,0:T(8,128)S(1)}, u32[]{:S(2)}, u32[]{:S(2)}) collective-permute-start(f32[96,128]{1,0:T(8,128)S(1)} %get-tuple-element.11), channel_id=1, source_target_pairs={{0,8},{8,0},{16,24},{24,16},{1,9},{9,1},{17,25},{25,17},{2,10},{10... | collective-permute-start | bytes 147464 | tf_op jit(solution)/shard_map/ppermute | solution.py:444
  37.3 0.5 collective-permute-done.7.rest_2_
  37.8 1.5 %collective-permute-done.5.rest_0_ = f32[96,128]{1,0:T(8,128)S(1)} collective-permute-done((f32[96,128]{1,0:T(8,128)S(1)}, f32[96,128]{1,0:T(8,128)S(1)}, u32[]{:S(2)}, u32[]{:S(2)}) %collective-permute-start.5) | collective-permute-done | bytes 49184 | tf_op jit(solution)/shard_map/ppermute | solution.py:444
  39.4 5.8 %near.3.close = f32[256,128]{1,0:T(8,128)S(1)} custom-call(s32[128]{0:T(128)S(1)} %copy-done.1, s32[128]{0:T(128)S(1)} %copy-done.2, f32[256,128]{1,0:T(8,128)S(1)} %get-tuple-element.10.pack, f32[96,128]{1,0:T(8,128)S(1)} %collective-permute-done.5.rest_0_, f32[96,128]{1,0:T(8,128)S(1)} %collective-permute-done.6.rest_1_, ...), custom_call_target="tpu_custom_call" | custom-call | tf_op jit(solution)/shard_map/near/pallas_call | solution.py:519
  45.1 0.0 copy-start.3
  45.2 0.6 %copy-done.3 = s32[32,1]{0,1:T(1,128)S(1)} copy-done((s32[32,1]{0,1:T(1,128)S(1)}, s32[32,1]{0,1:T(1,128)}, u32[]{:S(2)}) %copy-start.3) | copy-done | bytes 152
  45.8 2.2 %last_far.1 = f32[384,128]{1,0:T(8,128)S(1)} custom-call(s32[32]{0:T(128)S(1)} %bitcast.16, f32[256,128]{1,0:T(8,128)S(1)} %get-tuple-element.10.pack, f32[256,128]{1,0:T(8,128)S(1)} %near.3.close, f32[128,128]{1,0:T(8,128)S(1)} %bitcast.12, f32[56,128]{1,0:T(8,128)S(1)} %derivatives.1.table), custom_call_target="tpu_custom_call" | custom-call | tf_op jit(solution)/shard_map/last_far/pallas_call | solution.py:544
  48.0 13.1 %all_to_all.33 = f32[16,24,128]{2,1,0:T(8,128)S(1)} all-to-all(f32[16,24,128]{2,1,0:T(8,128)S(1)} %bitcast.10), channel_id=1, replica_groups=mesh['gx'=4,'gy'=4,'gz'=2] {'gx','gy'}, dimensions={0} | all-to-all | bytes 393216 | tf_op jit(solution)/shard_map/all_to_all | solution.py:555
  61.1 0.7 %receive.1 = (f32[3,64,128]{2,1,0:T(8,128)}, f32[3,64,128]{2,1,0:T(8,128)}) custom-call(f32[384,128]{1,0:T(8,128)S(1)} %bitcast.11), custom_call_target="tpu_custom_call" | custom-call | tf_op jit(solution)/shard_map/receive/pallas_call | solution.py:557
  (10 shorter events, 0.0 us)
Async XLA Ops:
  3.3 21.6 %all-to-all-start = ((f32[32,4,128]{2,1,0:T(4,128)}), f32[32,4,128]{2,1,0:T(4,128)S(1)}, u32[]{:S(2)}, u32[]{:S(2)}) async-start(f32[32,4,128]{2,1,0:T(4,128)} %bitcast.2), calls=%async_computation | async-start | bytes 131072 | tf_op jit(solution)/shard_map/all_to_all | solution.py:518
  10.6 8.5 %copy-start.1 = (s32[128]{0:T(128)S(1)}, s32[128]{0:T(128)}, u32[]{:S(2)}) copy-start(s32[128]{0:T(128)} %pair_targets.3) | copy-start | bytes 1540
  10.6 8.5 %copy-start.2 = (s32[128]{0:T(128)S(1)}, s32[128]{0:T(128)}, u32[]{:S(2)}) copy-start(s32[128]{0:T(128)} %pair_sources.3) | copy-start | bytes 1540
  10.6 6.5 %collective-permute-start.4 = (f32[96,128]{1,0:T(8,128)S(1)}, f32[96,128]{1,0:T(8,128)S(1)}, u32[]{:S(2)}, u32[]{:S(2)}) collective-permute-start(f32[96,128]{1,0:T(8,128)S(1)} %get-tuple-element.9), channel_id=1, source_target_pairs={{0,1},{1,0},{2,3},{3,2},{4,5},{5,4},{6,7},{7,6},{8,9},{9,8},{10,11... | collective-permute-start | bytes 147464 | tf_op jit(solution)/shard_map/ppermute | solution.py:444
  10.9 6.2 %collective-permute-start.3 = (f32[96,128]{1,0:T(8,128)S(1)}, f32[96,128]{1,0:T(8,128)S(1)}, u32[]{:S(2)}, u32[]{:S(2)}) collective-permute-start(f32[96,128]{1,0:T(8,128)S(1)} %get-tuple-element.9), channel_id=1, source_target_pairs={{0,1},{1,0},{2,4},{3,5},{4,2},{5,3},{6,7},{7,6},{8,9},{9,8},{10,12... | collective-permute-start | bytes 147464 | tf_op jit(solution)/shard_map/ppermute | solution.py:455
  11.2 6.3 %collective-permute-start.2 = (f32[96,128]{1,0:T(8,128)S(1)}, f32[96,128]{1,0:T(8,128)S(1)}, u32[]{:S(2)}, u32[]{:S(2)}) collective-permute-start(f32[96,128]{1,0:T(8,128)S(1)} %get-tuple-element.9), channel_id=1, source_target_pairs={{0,2},{2,0},{4,6},{6,4},{1,3},{3,1},{5,7},{7,5},{8,10},{10,8},{12,... | collective-permute-start | bytes 147464 | tf_op jit(solution)/shard_map/ppermute | solution.py:444
  14.0 3.5 %collective-permute-start.1 = (f32[96,128]{1,0:T(8,128)S(1)}, f32[96,128]{1,0:T(8,128)S(1)}, u32[]{:S(2)}, u32[]{:S(2)}) collective-permute-start(f32[96,128]{1,0:T(8,128)S(1)} %get-tuple-element.9), channel_id=1, source_target_pairs={{0,1},{1,0},{8,16},{9,17},{16,8},{17,9},{24,25},{25,24},{2,3},{3,2... | collective-permute-start | bytes 147464 | tf_op jit(solution)/shard_map/ppermute | solution.py:455
  14.0 5.0 %collective-permute-start = (f32[96,128]{1,0:T(8,128)S(1)}, f32[96,128]{1,0:T(8,128)S(1)}, u32[]{:S(2)}, u32[]{:S(2)}) collective-permute-start(f32[96,128]{1,0:T(8,128)S(1)} %get-tuple-element.9), channel_id=1, source_target_pairs={{0,8},{8,0},{16,24},{24,16},{1,9},{9,1},{17,25},{25,17},{2,10},{10... | collective-permute-start | bytes 147464 | tf_op jit(solution)/shard_map/ppermute | solution.py:444
  17.1 7.8 %copy-start = (s32[1536]{0:T(1024)S(1)}, s32[1536]{0:T(1024)}, u32[]{:S(2)}) copy-start(s32[1536]{0:T(1024)} %param.8) | copy-start | bytes 18436
  27.2 17.9 %all-to-all-start.1 = ((f32[32,4,128]{2,1,0:T(4,128)}), f32[32,4,128]{2,1,0:T(4,128)S(1)}, u32[]{:S(2)}, u32[]{:S(2)}) async-start(f32[32,4,128]{2,1,0:T(4,128)} %bitcast.4), calls=%async_computation.1 | async-start | bytes 131072 | tf_op jit(solution)/shard_map/all_to_all | solution.py:518
  30.9 6.4 %collective-permute-start.9 = (f32[96,128]{1,0:T(8,128)S(1)}, f32[96,128]{1,0:T(8,128)S(1)}, u32[]{:S(2)}, u32[]{:S(2)}) collective-permute-start(f32[96,128]{1,0:T(8,128)S(1)} %get-tuple-element.11), channel_id=1, source_target_pairs={{0,1},{1,0},{2,3},{3,2},{4,5},{5,4},{6,7},{7,6},{8,9},{9,8},{10,11... | collective-permute-start | bytes 147464 | tf_op jit(solution)/shard_map/ppermute | solution.py:444
  31.3 6.1 %collective-permute-start.8 = (f32[96,128]{1,0:T(8,128)S(1)}, f32[96,128]{1,0:T(8,128)S(1)}, u32[]{:S(2)}, u32[]{:S(2)}) collective-permute-start(f32[96,128]{1,0:T(8,128)S(1)} %get-tuple-element.11), channel_id=1, source_target_pairs={{0,1},{1,0},{2,4},{3,5},{4,2},{5,3},{6,7},{7,6},{8,9},{9,8},{10,12... | collective-permute-start | bytes 147464 | tf_op jit(solution)/shard_map/ppermute | solution.py:455
  31.5 6.3 %collective-permute-start.7 = (f32[96,128]{1,0:T(8,128)S(1)}, f32[96,128]{1,0:T(8,128)S(1)}, u32[]{:S(2)}, u32[]{:S(2)}) collective-permute-start(f32[96,128]{1,0:T(8,128)S(1)} %get-tuple-element.11), channel_id=1, source_target_pairs={{0,2},{2,0},{4,6},{6,4},{1,3},{3,1},{5,7},{7,5},{8,10},{10,8},{12,... | collective-permute-start | bytes 147464 | tf_op jit(solution)/shard_map/ppermute | solution.py:444
  34.4 3.5 %collective-permute-start.6 = (f32[96,128]{1,0:T(8,128)S(1)}, f32[96,128]{1,0:T(8,128)S(1)}, u32[]{:S(2)}, u32[]{:S(2)}) collective-permute-start(f32[96,128]{1,0:T(8,128)S(1)} %get-tuple-element.11), channel_id=1, source_target_pairs={{0,1},{1,0},{8,16},{9,17},{16,8},{17,9},{24,25},{25,24},{2,3},{3,2... | collective-permute-start | bytes 147464 | tf_op jit(solution)/shard_map/ppermute | solution.py:455
  34.4 5.0 %collective-permute-start.5 = (f32[96,128]{1,0:T(8,128)S(1)}, f32[96,128]{1,0:T(8,128)S(1)}, u32[]{:S(2)}, u32[]{:S(2)}) collective-permute-start(f32[96,128]{1,0:T(8,128)S(1)} %get-tuple-element.11), channel_id=1, source_target_pairs={{0,8},{8,0},{16,24},{24,16},{1,9},{9,1},{17,25},{25,17},{2,10},{10... | collective-permute-start | bytes 147464 | tf_op jit(solution)/shard_map/ppermute | solution.py:444
  45.1 0.7 %copy-start.3 = (s32[32,1]{0,1:T(1,128)S(1)}, s32[32,1]{0,1:T(1,128)}, u32[]{:S(2)}) copy-start(s32[32,1]{0,1:T(1,128)} %param.11) | copy-start | bytes 388

commit v2 on v1

--- a/solution.py
+++ b/solution.py
@@ -14,7 +14,9 @@
 LANES = 128
 ROWS = 8
 FEATURES = 32
-BATCH = 16
+BATCH = 128
+LEAD = 12
+LAG = 8
 
 core_sq = 0.0025
 time_step = 0.1
@@ -67,7 +69,7 @@
     ]
 
 
-def moments_kernel(tiles, devices, pack, leaf, work, line):
+def leaf_moments(pack, tiles, devices, copies, work, line):
     middle_x, middle_y, _ = slab_middle(1)
     middle = (middle_x, middle_y, 0.5)
     low = row_ids() < 4
@@ -114,9 +116,9 @@
         summed = jnp.sum(both.T, axis=0, keepdims=True)
         line[k : k + 1, 0:TERMS] = summed
         line[k + 4 : k + 5, 0:TERMS] = summed
-    copies = line[...]
+    both = line[...]
     for at in range(devices * 4 // ROWS):
-        leaf[at * ROWS : (at + 1) * ROWS, :] = copies
+        copies[at * ROWS : (at + 1) * ROWS, :] = both
 
 
 def pick_ghosts(pack, tiles, ghost_ids, ghosts):
@@ -132,7 +134,29 @@
         ghosts[out_tile * ROWS : (out_tile + 1) * ROWS, :] = found
 
 
-def prologue_kernel(tiles, deep, offsets_in, strength_in, ids_in, pack, ghosts, offsets, strength, ghost_ids, arrivals):
+def pick_positions(pack, tiles, ghost_ids, ghosts):
+    low = row_ids() < 4
+    pairs = ghost_ids.shape[0] // 2
+    lanes, owner, found = [], [], []
+    for pair in range(pairs):
+        wanted = jnp.where(low, spread(ghost_ids, 2 * pair), spread(ghost_ids, 2 * pair + 1))
+        lanes.append(wanted & (LANES - 1))
+        owner.append(wanted >> 7)
+        found.append(jnp.zeros((ROWS, LANES), f32))
+    for tile in range(tiles):
+        value = pack[tile * ROWS : (tile + 1) * ROWS, :]
+        value = jnp.where(low, value, pltpu.roll(value, 4, 0))
+        for pair in range(pairs):
+            moved = jnp.take_along_axis(value, lanes[pair], axis=1, mode="promise_in_bounds")
+            found[pair] = jnp.where(owner[pair] == tile, moved, found[pair])
+    for pair in range(pairs):
+        ghosts[pair * ROWS : (pair + 1) * ROWS, :] = found[pair]
+
+
+def prologue_kernel(
+    tiles, devices, deep, offsets_in, strength_in, ids_in, pack, ghosts, leaf,
+    offsets, strength, ghost_ids, arrivals, copies, leaving, work, line,
+):
     loads = [
         pltpu.make_async_copy(source, target, arrivals.at[number])
         for number, (source, target) in enumerate(
@@ -161,7 +185,11 @@
         pack[base + 3 : base + 4, :] = blank
         pack[base + 4 : base + 7, :] = strength[:, span]
         pack[base + 7 : base + 8, :] = blank
+    leaf_moments(pack, tiles, devices, copies, work, line)
+    store = pltpu.make_async_copy(copies, leaf, leaving.at[0])
+    store.start()
     pick_ghosts(pack, tiles, ghost_ids, ghosts)
+    store.wait()
 
 
 def derivative_kernel(wide, tall, deep, table):
@@ -259,9 +287,34 @@
     store_features(place, targets, [join(one, two), join(one, two), join(three, one), sizes])
 
 
-def near_kernel(tiles, ghost_tiles, deep, beside, pair_targets, pair_sources, pack, *rest):
-    ghost_in = rest[: 2 * len(beside)]
-    close, sources, targets, pushes, near = rest[2 * len(beside) :]
+def block_placer(owners, group, capacity):
+    blocks = owners.shape[1]
+    own = owners[...].astype(f32)
+    down = lax.broadcasted_iota(jnp.int32, (blocks, blocks), 0)
+    along = lax.broadcasted_iota(jnp.int32, (blocks, blocks), 1)
+    wide = jnp.broadcast_to(own, (blocks, blocks))
+    tall = jnp.sum(jnp.where(down == along, wide, 0.0), axis=1, keepdims=True)
+    earlier = jnp.where((wide == tall) & (down < along), 1.0, 0.0)
+    slot = own * float(capacity) + jnp.sum(earlier, axis=0, keepdims=True)
+    place = lax.broadcasted_iota(jnp.int32, (group * capacity, blocks), 0).astype(f32)
+    return jnp.where(place == slot, 1.0, 0.0).astype(bf16)
+
+
+def near_kernel(
+    tiles, ghost_tiles, deep, beside, targets_in, sources_in, pack, *rest
+):
+    count = 2 * len(beside)
+    ghost_in, strength_in, rest = rest[:count], rest[count : 2 * count], rest[2 * count :]
+    halved = ghost_in[0].shape[0] < strength_in[0].shape[0]
+    close, sources, targets, pushes, near, pair_targets, pair_sources, arrivals = rest
+    loads = [
+        pltpu.make_async_copy(source, target, arrivals.at[number])
+        for number, (source, target) in enumerate(
+            ((targets_in, pair_targets), (sources_in, pair_sources))
+        )
+    ]
+    for load in loads:
+        load.start()
     row = row_ids()
     middle = slab_middle(deep)
 
@@ -276,52 +329,68 @@
         index = lax.axis_index(name)
         odd = lax.rem(index, 2) == 1
         has_lower, has_upper = index > 0, index < count - 1
-        from_a, from_b = ghost_in[2 * number], ghost_in[2 * number + 1]
-
-        def ghost_tile(tile, carry, number=number, odd=odd, lows=has_lower, ups=has_upper, a=from_a, b=from_b):
-            one, other = tile_of(a, tile), tile_of(b, tile)
-            base = tiles + 2 * number * ghost_tiles + tile
-            for which, (value, present) in enumerate(
-                ((jnp.where(odd, one, other), lows), (jnp.where(odd, other, one), ups))
-            ):
-                value = jnp.where((row < 4) | present, value, 0.0)
-                source_features(value, middle, base + which * ghost_tiles, sources, pushes)
+
+        def ghost_pair(pair, carry, number=number, odd=odd, lows=has_lower, ups=has_upper):
+            for which, present in enumerate((lows, ups)):
+                def held(refs, tile):
+                    one, other = tile_of(refs[2 * number], tile), tile_of(refs[2 * number + 1], tile)
+                    return jnp.where(odd, other, one) if which else jnp.where(odd, one, other)
+
+                base = tiles + (2 * number + which) * ghost_tiles
+                if halved:
+                    both = held(ghost_in, pair)
+                for half in range(2):
+                    tile = 2 * pair + half
+                    value = held(strength_in, tile)
+                    if halved:
+                        value = jnp.where(row < 4, pltpu.roll(both, 4, 0) if half else both, value)
+                    value = jnp.where((row < 4) | present, value, 0.0)
+                    source_features(value, middle, base + tile, sources, pushes)
             return carry
 
-        lax.fori_loop(0, ghost_tiles, ghost_tile, 0)
+        lax.fori_loop(0, ghost_tiles // 2, ghost_pair, 0)
 
     near[...] = jnp.zeros_like(near)
+    for load in loads:
+        load.wait()
     pair_count = pair_targets.shape[0]
     batch = BATCH if pair_count % BATCH == 0 else 1
 
     def batch_of_pairs(number, carry):
         names = [(pair_targets[number * batch + at], pair_sources[number * batch + at]) for at in range(batch)]
-        gaps = [
-            lax.dot_general(
+
+        def gap_of(at):
+            here, there = names[at]
+            return lax.dot_general(
                 sources[pl.ds(pl.multiple_of(there * FEATURES, FEATURES), FEATURES), :],
                 targets[pl.ds(pl.multiple_of(here * FEATURES, FEATURES), FEATURES), :],
                 (((0,), (0,)), ((), ())),
                 preferred_element_type=f32,
             )
-            for here, there in names
-        ]
-        weights = []
-        for gap in gaps:
+
+        def gain_of(at, gap):
+            there = names[at][1]
             kernel_block = lax.rsqrt(jnp.maximum(gap, core_sq))
             coarse = kernel_block.astype(bf16)
             fine = (kernel_block - coarse.astype(f32)).astype(bf16)
-            weights.append(jnp.concatenate([coarse, fine], axis=0))
-        gains = [
-            jnp.dot(
+            return jnp.dot(
                 pushes[pl.ds(pl.multiple_of(there * 2 * ROWS, 2 * ROWS), 2 * ROWS), :],
-                weight,
+                jnp.concatenate([coarse, fine], axis=0),
                 preferred_element_type=f32,
             )
-            for (here, there), weight in zip(names, weights)
-        ]
-        for (here, there), gain in zip(names, gains):
-            spot = pl.ds(pl.multiple_of(here * 2 * ROWS, 2 * ROWS), 2 * ROWS)
+
+        def add(at, gain):
+            spot = pl.ds(pl.multiple_of(names[at][0] * 2 * ROWS, 2 * ROWS), 2 * ROWS)
             near[spot, :] = near[spot, :] + gain
+
+        gaps, gains = {}, {}
+        for at in range(batch + LEAD + LAG):
+            if at < batch:
+                gaps[at] = gap_of(at)
+            if 0 <= at - LEAD < batch:
+                gains[at - LEAD] = gain_of(at - LEAD, gaps.pop(at - LEAD))
+            if 0 <= at - LEAD - LAG < batch:
+                add(at - LEAD - LAG, gains.pop(at - LEAD - LAG))
         return carry
 
     lax.fori_loop(0, pair_count // batch, batch_of_pairs, 0)
@@ -338,11 +407,11 @@
 def far_kernel(tiles, wide, tall, deep, final, capacity, chosen, pack, close, received, table, *rest):
     columns = wide * tall
     if final:
-        owners = chosen
-        sent, pack_out, speed, work, expansion, square, slots, counts = rest
+        sent, moved, speed, work, expansion, square, owners, arrival = rest
+        load = pltpu.make_async_copy(chosen, owners, arrival.at[0])
+        load.start()
     else:
-        ghost_ids = chosen
-        pack_out, ghosts, speed, work, expansion, square = rest
+        pack_out, ghosts, leaf, speed, work, expansion, square, copies, leaving, line = rest
     row = row_ids()
     middle = slab_middle(deep)
 
@@ -390,71 +459,68 @@
     def advance(tile, carry):
         place = pl.ds(pl.multiple_of(tile * ROWS, ROWS), ROWS)
         velocity = jnp.where(row < 3, close[place, :] + speed[place, :], 0.0)
-        speed[place, :] = velocity
-        pack_out[place, :] = pack[place, :] + time_step * velocity
+        later = pack[place, :] + time_step * velocity
+        if final:
+            moved[place, :] = jnp.where(row < 3, later, pltpu.roll(velocity, 3, 0))
+        else:
+            pack_out[place, :] = later
         return carry
 
     lax.fori_loop(0, tiles, advance, 0, unroll=4)
 
     if not final:
-        pick_ghosts(pack_out, tiles, ghost_ids, ghosts)
+        leaf_moments(pack_out, tiles, wide * tall * deep, copies, work, line)
+        store = pltpu.make_async_copy(copies, leaf, leaving.at[0])
+        store.start()
+        pick_positions(pack_out, tiles, chosen, ghosts)
+        store.wait()
         return
 
     group = wide * tall
-    blank = jnp.zeros((ROWS, LANES), f32)
-    pack_out[tiles * ROWS : (tiles + 1) * ROWS, :] = blank
-    speed[tiles * ROWS : (tiles + 1) * ROWS, :] = blank
-
-    def clear_slot(at, carry):
-        slots[at] = tiles
-        return carry
-
-    def clear_count(at, carry):
-        counts[at] = 0
-        return carry
-
-    def assign(block, carry):
-        owner = owners[block]
-        earlier = counts[owner]
-        counts[owner] = earlier + 1
-        slots[owner * capacity + earlier] = block
-        return carry
-
-    lax.fori_loop(0, group * capacity, clear_slot, 0)
-    lax.fori_loop(0, group, clear_count, 0)
-    lax.fori_loop(0, tiles, assign, 0)
-    for at in range(group * capacity):
-        block = slots[at]
-        sent[at * 6 : at * 6 + 3, :] = tile_of(pack_out, block)[0:3, :]
-        sent[at * 6 + 3 : at * 6 + 6, :] = tile_of(speed, block)[0:3, :]
-
-
-def receive_kernel(handed, positions, velocity):
-    count = positions.shape[1]
-    for axis in range(3):
-        positions[axis] = handed[pl.ds(axis, count, stride=6), :]
-        velocity[axis] = handed[pl.ds(axis + 3, count, stride=6), :]
-
-
-def swap_neighbours(block, name):
+    load.wait()
+    placer = block_placer(owners, group, capacity)
+    placer = jnp.concatenate([placer] * 3, axis=1)
+    for field in range(6):
+        values = split_three(moved[pl.ds(field, tiles, stride=ROWS), :])
+        values = jnp.concatenate([value.astype(bf16) for value in values], axis=0)
+        placed = jnp.dot(placer, values, preferred_element_type=f32)
+        for owner in range(group):
+            base = (owner * 6 + field) * capacity
+            sent[base : base + capacity, :] = placed[owner * capacity : (owner + 1) * capacity, :]
+
+
+def receive_kernel(capacity, handed, positions, velocity):
+    for sender in range(positions.shape[1] // capacity):
+        slots = slice(sender * capacity, (sender + 1) * capacity)
+        for axis in range(3):
+            base = (sender * 6 + axis) * capacity
+            positions[axis, slots, :] = handed[base : base + capacity, :]
+            base = base + 3 * capacity
+            velocity[axis, slots, :] = handed[base : base + capacity, :]
+
+
+def even_pairs(block, name):
     count = lax.axis_size(name)
     if count == 1:
-        return block, block
-    even = [(i, i ^ 1) for i in range(count)]
-    first = lax.ppermute(block, name, even)
-    if count == 2:
-        return first, first
-    deep = lax.axis_size("gz")
-    if name != "gz" and deep % 2 == 0:
-        odd = []
-        for i in range(count):
-            for k in range(deep):
-                end = i in (0, count - 1)
-                other = i * deep + (k ^ 1) if end else (i + 1 if i % 2 else i - 1) * deep + k
-                odd.append((i * deep + k, other))
-        return first, lax.ppermute(block, (name, "gz"), odd)
-    odd = [(i, (i + 1) % count if i % 2 else (i - 1) % count) for i in range(count)]
-    return first, lax.ppermute(block, name, odd)
+        return block
+    return lax.ppermute(block, name, [(i, i ^ 1) for i in range(count)])
+
+
+def odd_pairs(block, name):
+    count, deep = lax.axis_size(name), lax.axis_size("gz")
+    if count <= 2:
+        return block
+    if name == "gz" or deep % 2:
+        return lax.ppermute(
+            block, name, [(i, (i + 1) % count if i % 2 else (i - 1) % count) for i in range(count)]
+        )
+    moves = []
+    for i in range(count):
+        for k in range(deep):
+            end = i in (0, count - 1)
+            other = i * deep + (k ^ 1) if end else (i + 1 if i % 2 else i - 1) * deep + k
+            moves.append((i * deep + k, other))
+    return lax.ppermute(block, (name, "gz"), moves)
 
 
 def per_device(offsets, strength, ghost_list, pair_targets, pair_sources, owners):
@@ -466,7 +532,6 @@
     capacity = max(2, 2 * tiles // group)
     ghost_ids = ghost_list.reshape(ghost_tiles, LANES)
     in_vmem = pl.BlockSpec(memory_space=pltpu.VMEM)
-    in_smem = pl.BlockSpec(memory_space=pltpu.SMEM)
     pack_type = jax.ShapeDtypeStruct((tiles * ROWS, LANES), f32)
     leaf_type = jax.ShapeDtypeStruct((devices * 4, LANES), f32)
     ghost_type = jax.ShapeDtypeStruct((ghost_tiles * ROWS, LANES), f32)
@@ -475,21 +540,29 @@
     params = pltpu.CompilerParams(vmem_limit_bytes=48 << 20)
 
     in_place = pl.BlockSpec(memory_space=pltpu.HBM)
-
-    pack, ghosts = pl.pallas_call(
-        functools.partial(prologue_kernel, tiles, deep),
-        out_shape=(pack_type, ghost_type),
+    in_hbm = functools.partial(pltpu.with_memory_space_constraint, memory_space=pltpu.HBM)
+
+    copies = pltpu.VMEM((devices * 4, LANES), f32)
+    one_copy = pltpu.SemaphoreType.DMA((1,))
+
+    pack, ghosts, leaf = pl.pallas_call(
+        functools.partial(prologue_kernel, tiles, devices, deep),
+        out_shape=(pack_type, ghost_type, leaf_type),
         in_specs=[in_place] * 3,
-        out_specs=(in_vmem,) * 2,
+        out_specs=(in_vmem, in_vmem, in_place),
         scratch_shapes=[
             pltpu.VMEM(offsets.shape, f32),
             pltpu.VMEM(strength.shape, f32),
             pltpu.VMEM(ghost_ids.shape, jnp.int32),
             pltpu.SemaphoreType.DMA((3,)),
+            copies,
+            one_copy,
+            work,
+            line,
         ],
         compiler_params=params,
         name="prologue",
-    )(*(pltpu.with_memory_space_constraint(value, pltpu.HBM) for value in (offsets, strength, ghost_ids)))
+    )(in_hbm(offsets), in_hbm(strength), in_hbm(ghost_ids))
     table = pl.pallas_call(
         functools.partial(derivative_kernel, wide, tall, deep),
         out_shape=jax.ShapeDtypeStruct((TERMS, LANES), f32),
@@ -499,63 +572,61 @@
     )()
     beside = tuple((name, lax.axis_size(name)) for name in everywhere)
     places = tiles + 2 * len(beside) * ghost_tiles
-    taller = pltpu.VMEM(((tiles + 1) * ROWS, LANES), f32)
     for step_number in range(2):
         final = step_number == 1
         arrived = []
-        for name, count in beside:
-            arrived.extend(swap_neighbours(ghosts, name))
-        leaf = pl.pallas_call(
-            functools.partial(moments_kernel, tiles, devices),
-            out_shape=leaf_type,
-            in_specs=[in_vmem],
-            out_specs=in_vmem,
-            scratch_shapes=[work, line],
-            compiler_params=params,
-            name="moments",
-        )
-        leaf = leaf(pack)
+        for name, _ in beside:
+            arrived.extend((even_pairs(ghosts, name), odd_pairs(ghosts, name)))
+        if not final:
+            strengths = arrived
         received = lax.all_to_all(leaf, everywhere, split_axis=0, concat_axis=0, tiled=True)
         close = pl.pallas_call(
             functools.partial(near_kernel, tiles, ghost_tiles, deep, beside),
             out_shape=pack_type,
-            in_specs=[in_smem] * 2 + [in_vmem] * (1 + len(arrived)),
+            in_specs=[in_place] * 2 + [in_vmem] * (1 + 2 * len(arrived)),
             out_specs=in_vmem,
             scratch_shapes=[
                 pltpu.VMEM((places * FEATURES, LANES), bf16),
                 pltpu.VMEM((tiles * FEATURES, LANES), bf16),
                 pltpu.VMEM((places * 2 * ROWS, 2 * LANES), bf16),
                 pltpu.VMEM((tiles * 2 * ROWS, LANES), f32),
+                pltpu.SMEM(pair_targets.shape, jnp.int32),
+                pltpu.SMEM(pair_sources.shape, jnp.int32),
+                pltpu.SemaphoreType.DMA((2,)),
             ],
             compiler_params=params,
             name="near",
-        )(pair_targets, pair_sources, pack, *arrived)
+        )(in_hbm(pair_targets), in_hbm(pair_sources), pack, *arrived, *strengths)
+        speed, square = pltpu.VMEM((tiles * ROWS, LANES), f32), pltpu.VMEM((LANES, LANES), f32)
         if final:
+            chosen = in_hbm(owners.reshape(1, tiles))
             out_shape = jax.ShapeDtypeStruct((group * capacity * 6, LANES), f32)
             out_specs = in_vmem
-            extra = [taller, taller, work, work, pltpu.VMEM((LANES, LANES), f32)] + [
-                pltpu.SMEM((group * capacity,), jnp.int32),
-                pltpu.SMEM((group,), jnp.int32),
+            extra = [
+                pltpu.VMEM((tiles * ROWS, LANES), f32), speed, work, work, square,
+                pltpu.VMEM((1, tiles), jnp.int32), one_copy,
             ]
         else:
-            out_shape = (pack_type, ghost_type)
-            out_specs = (in_vmem,) * 2
-            extra = [taller, work, work, pltpu.VMEM((LANES, LANES), f32)]
+            chosen = ghost_ids
+            half_type = jax.ShapeDtypeStruct((ghost_tiles * 4, LANES), f32)
+            out_shape = (pack_type, half_type, leaf_type)
+            out_specs = (in_vmem, in_vmem, in_place)
+            extra = [speed, work, work, square, copies, one_copy, line]
         result = pl.pallas_call(
             functools.partial(far_kernel, tiles, wide, tall, deep, final, capacity),
             out_shape=out_shape,
-            in_specs=[in_smem if final else in_vmem] + [in_vmem] * 4,
+            in_specs=[in_place if final else in_vmem] + [in_vmem] * 4,
             out_specs=out_specs,
             scratch_shapes=extra,
             compiler_params=params,
             name="last_far" if final else "far",
-        )(owners[:, 0] if final else ghost_ids, pack, close, received, table)
+        )(chosen, pack, close, received, table)
         if not final:
-            pack, ghosts = result
+            pack, ghosts, leaf = result
     handed = lax.all_to_all(result, ("gx", "gy"), split_axis=0, concat_axis=0, tiled=True)
     moved = jax.ShapeDtypeStruct((3, group * capacity, LANES), f32)
     moved = pl.pallas_call(
-        receive_kernel,
+        functools.partial(receive_kernel, capacity),
         out_shape=(moved, moved),
         in_specs=[in_vmem],
         out_specs=(in_vmem,) * 2,

time: 62.1 us -> 52.8 us (0.85)
  Pallas kernels: 19.5 us -> 11.6 us
  local copies, waits for them, and re-layouts: 0.67 us -> 0.01 us
    pallas_call x2, Pallas kernels: 11.5 us -> 5.72 us  [per_device(): pl.pallas_call(functools.partial(near_kernel, tiles, ghost_tiles, deep, b...]
    pallas_call x4 -> x2, Pallas kernels: 4.48 us -> 2.87 us  [the longest x1 2.16 us: per_device(): pl.pallas_call(functools.partial(prologue_kernel, tiles, devices, deep),...]
    unnamed x8 -> x2, local copies, waits for them, and re-layouts: 0.67 us -> 0.01 us
  transfers between devices with their start and end apart: 12 -> 12, of which waited for: 4 -> 3; matrix products, arithmetic and copies ran while one was open for 0% -> 0% of each run, Pallas kernels for 19% -> 11%
where the time goes in v2:
time: 52.8 us; the launch traced here: 52.5 us
  starting transfers between devices  23.8 us (45%)
  blocking collectives  12.6 us (24%)
  Pallas kernels  11.6 us (22%)
  waiting for transfers between devices  3.75 us (7%)
  between operations  0.75 us (1%)
    all_to_all x1, blocking collectives, per_device(): lax.all_to_all(result, ('gx', 'gy'), split_axis=0, concat_axis=0, tiled=T...  12.6 us
    ppermute x6, starting transfers between devices, even_pairs(): return lax.ppermute(block, name, [(i, i ^ 1) for i in range(count)])  12.2 us
    all_to_all x2, starting transfers between devices, per_device(): lax.all_to_all(leaf, everywhere, split_axis=0, concat_axis=0, tiled=True)  11.1 us
    pallas_call x2, Pallas kernels, per_device(): pl.pallas_call(functools.partial(near_kernel, tiles, ghost_tiles, deep, b...  5.72 us
    ppermute x6, waiting for transfers between devices, even_pairs(): return lax.ppermute(block, name, [(i, i ^ 1) for i in range(count)])  3.74 us
    pallas_call x2, Pallas kernels, per_device(): pl.pallas_call(functools.partial(far_kernel, tiles, wide, tall, deep, fin...  2.94 us
    pallas_call x1, Pallas kernels, per_device(): pl.pallas_call(functools.partial(prologue_kernel, tiles, devices, deep),...  2.16 us
  transfers between devices with their start and end apart: 12, of which 3 were waited for; matrix products, arithmetic and copies ran while one was open for 0% of the time, Pallas kernels for 11%

profile of v2, /device:TPU:0, one launch (start us, length us, event | category | flops | bytes accessed | tf_op | source)
XLA Modules:
  0.0 52.5 jit_solution(7317367556095594036)
XLA Ops:
  0.6 2.2 %prologue.1 = (f32[256,128]{1,0:T(8,128)S(1)}, f32[96,128]{1,0:T(8,128)S(1)}, f32[128,128]{1,0:T(8,128)}) custom-call(f32[3,4096]{1,0:T(4,128)} %offsets_in.1, f32[3,4096]{1,0:T(4,128)} %strength_in.1, s32[12,128]{1,0:T(8,128)} %bitcast.14), custom_call_target="tpu_custom_call" | custom-call | tf_op jit(solution)/shard_map/prologue/pallas_call | solution.py:548
  2.8 7.3 %all-to-all-start = ((f32[32,4,128]{2,1,0:T(4,128)}), f32[32,4,128]{2,1,0:T(4,128)S(1)}, u32[]{:S(2)}, u32[]{:S(2)}) async-start(f32[32,4,128]{2,1,0:T(4,128)} %bitcast.2), calls=%async_computation | async-start | bytes 131072 | tf_op jit(solution)/shard_map/all_to_all | solution.py:582
  10.1 0.3 collective-permute-start.4
  10.5 0.3 collective-permute-start.3
  10.7 2.8 %collective-permute-start.2 = (f32[96,128]{1,0:T(8,128)S(1)}, f32[96,128]{1,0:T(8,128)S(1)}, u32[]{:S(2)}, u32[]{:S(2)}) collective-permute-start(f32[96,128]{1,0:T(8,128)S(1)} %get-tuple-element.11.rest_5_.rest_11_), channel_id=1, source_target_pairs={{0,2},{2,0},{4,6},{6,4},{1,3},{3,1},{5,7},{7,5},{8,10},{10,8},{12,... | collective-permute-start | bytes 147464 | tf_op jit(solution)/shard_map/ppermute | solution.py:506
  13.5 0.0 collective-permute-start.1
  13.6 3.0 %collective-permute-start = (f32[96,128]{1,0:T(8,128)S(1)}, f32[96,128]{1,0:T(8,128)S(1)}, u32[]{:S(2)}, u32[]{:S(2)}) collective-permute-start(f32[96,128]{1,0:T(8,128)S(1)} %get-tuple-element.11.rest_5_.rest_11_), channel_id=1, source_target_pairs={{0,8},{8,0},{16,24},{24,16},{1,9},{9,1},{17,25},{25,17},{2,10},{10... | collective-permute-start | bytes 147464 | tf_op jit(solution)/shard_map/ppermute | solution.py:506
  16.5 0.1 derivatives.1.table
  16.6 0.0 collective-permute-done.4.rest_4_.rest_10_
  16.6 0.0 collective-permute-done.3.rest_3_.rest_9_
  16.6 0.4 collective-permute-done.2.rest_2_.rest_8_
  17.0 0.0 collective-permute-done.1.rest_1_.rest_7_
  17.0 1.5 %collective-permute-done.rest_0_.rest_6_ = f32[96,128]{1,0:T(8,128)S(1)} collective-permute-done((f32[96,128]{1,0:T(8,128)S(1)}, f32[96,128]{1,0:T(8,128)S(1)}, u32[]{:S(2)}, u32[]{:S(2)}) %collective-permute-start) | collective-permute-done | bytes 49184 | tf_op jit(solution)/shard_map/ppermute | solution.py:506
  18.6 2.9 %near.2.close = f32[256,128]{1,0:T(8,128)S(1)} custom-call(s32[128]{0:T(128)} %targets_in.3, s32[128]{0:T(128)} %sources_in.3, f32[256,128]{1,0:T(8,128)S(1)} %get-tuple-element.10.pack, f32[96,128]{1,0:T(8,128)S(1)} %collective-permute-done.rest_0_.rest_6_, f32[96,128]{1,0:T(8,128)S(1)} %collective-permute-done.1.rest_1_.rest_7_, ...), custom_call_target="tpu_custom_call" | custom-call | tf_op jit(solution)/shard_map/near/pallas_call | solution.py:583
  21.4 0.0 all-to-all-done
  21.5 1.9 %far.1 = (f32[256,128]{1,0:T(8,128)S(1)}, f32[48,128]{1,0:T(8,128)S(1)}, f32[128,128]{1,0:T(8,128)}) custom-call(s32[12,128]{1,0:T(8,128)S(1)} %bitcast.15, f32[256,128]{1,0:T(8,128)S(1)} %get-tuple-element.10.pack, f32[256,128]{1,0:T(8,128)S(1)} %near.2.close, f32[128,128]{1,0:T(8,128)S(1)} %bitcast.13, f32[56,128]{1,0:T(8,128)S(1)} %derivatives.1.table), custom_call_target="tpu_custom_call" | custom-call | tf_op jit(solution)/shard_map/far/pallas_call | solution.py:615
  23.4 3.7 %all-to-all-start.1 = ((f32[32,4,128]{2,1,0:T(4,128)}), f32[32,4,128]{2,1,0:T(4,128)S(1)}, u32[]{:S(2)}, u32[]{:S(2)}) async-start(f32[32,4,128]{2,1,0:T(4,128)} %bitcast.4), calls=%async_computation.1 | async-start | bytes 131072 | tf_op jit(solution)/shard_map/all_to_all | solution.py:582
  27.1 0.3 collective-permute-start.9
  27.5 0.3 collective-permute-start.8
  27.7 2.8 %collective-permute-start.7 = (f32[48,128]{1,0:T(8,128)S(1)}, f32[48,128]{1,0:T(8,128)S(1)}, u32[]{:S(2)}, u32[]{:S(2)}) collective-permute-start(f32[48,128]{1,0:T(8,128)S(1)} %get-tuple-element.14.rest_5_), channel_id=1, source_target_pairs={{0,2},{2,0},{4,6},{6,4},{1,3},{3,1},{5,7},{7,5},{8,10},{10,8},{12,... | collective-permute-start | bytes 73736 | tf_op jit(solution)/shard_map/ppermute | solution.py:506
  30.6 0.0 collective-permute-start.6
  30.6 3.0 %collective-permute-start.5 = (f32[48,128]{1,0:T(8,128)S(1)}, f32[48,128]{1,0:T(8,128)S(1)}, u32[]{:S(2)}, u32[]{:S(2)}) collective-permute-start(f32[48,128]{1,0:T(8,128)S(1)} %get-tuple-element.14.rest_5_), channel_id=1, source_target_pairs={{0,8},{8,0},{16,24},{24,16},{1,9},{9,1},{17,25},{25,17},{2,10},{10... | collective-permute-start | bytes 73736 | tf_op jit(solution)/shard_map/ppermute | solution.py:506
  33.5 0.0 collective-permute-done.9.rest_4_
  33.5 0.0 collective-permute-done.8.rest_3_
  33.5 0.0 collective-permute-done.7.rest_2_
  33.5 0.0 collective-permute-done.6.rest_1_
  33.5 1.8 %collective-permute-done.5.rest_0_ = f32[48,128]{1,0:T(8,128)S(1)} collective-permute-done((f32[48,128]{1,0:T(8,128)S(1)}, f32[48,128]{1,0:T(8,128)S(1)}, u32[]{:S(2)}, u32[]{:S(2)}) %collective-permute-start.5) | collective-permute-done | bytes 24608 | tf_op jit(solution)/shard_map/ppermute | solution.py:506
  35.3 2.9 %near.3.close = f32[256,128]{1,0:T(8,128)S(1)} custom-call(s32[128]{0:T(128)} %targets_in.3, s32[128]{0:T(128)} %sources_in.3, f32[256,128]{1,0:T(8,128)S(1)} %get-tuple-element.13.pack, f32[48,128]{1,0:T(8,128)S(1)} %collective-permute-done.5.rest_0_, f32[48,128]{1,0:T(8,128)S(1)} %collective-permute-done.6.rest_1_, ...), custom_call_target="tpu_custom_call" | custom-call | tf_op jit(solution)/shard_map/near/pallas_call | solution.py:583
  38.2 0.0 all-to-all-done.1
  38.2 1.0 %last_far.1 = f32[384,128]{1,0:T(8,128)S(1)} custom-call(s32[1,32]{1,0:T(1,128)} %bitcast.16, f32[256,128]{1,0:T(8,128)S(1)} %get-tuple-element.13.pack, f32[256,128]{1,0:T(8,128)S(1)} %near.3.close, f32[128,128]{1,0:T(8,128)S(1)} %bitcast.12, f32[56,128]{1,0:T(8,128)S(1)} %derivatives.1.table), custom_call_target="tpu_custom_call" | custom-call | tf_op jit(solution)/shard_map/last_far/pallas_call | solution.py:615
  39.2 12.6 %all_to_all.33 = f32[16,24,128]{2,1,0:T(8,128)S(1)} all-to-all(f32[16,24,128]{2,1,0:T(8,128)S(1)} %bitcast.10), channel_id=1, replica_groups=mesh['gx'=4,'gy'=4,'gz'=2] {'gx','gy'}, dimensions={0} | all-to-all | bytes 393216 | tf_op jit(solution)/shard_map/all_to_all | solution.py:626
  51.8 0.7 %receive.1 = (f32[3,64,128]{2,1,0:T(8,128)}, f32[3,64,128]{2,1,0:T(8,128)}) custom-call(f32[384,128]{1,0:T(8,128)S(1)} %bitcast.11), custom_call_target="tpu_custom_call" | custom-call | tf_op jit(solution)/shard_map/receive/pallas_call | solution.py:628
  (2 shorter events, 0.0 us)
Async XLA Ops:
  2.8 18.6 %all-to-all-start = ((f32[32,4,128]{2,1,0:T(4,128)}), f32[32,4,128]{2,1,0:T(4,128)S(1)}, u32[]{:S(2)}, u32[]{:S(2)}) async-start(f32[32,4,128]{2,1,0:T(4,128)} %bitcast.2), calls=%async_computation | async-start | bytes 131072 | tf_op jit(solution)/shard_map/all_to_all | solution.py:582
  10.1 6.5 %collective-permute-start.4 = (f32[96,128]{1,0:T(8,128)S(1)}, f32[96,128]{1,0:T(8,128)S(1)}, u32[]{:S(2)}, u32[]{:S(2)}) collective-permute-start(f32[96,128]{1,0:T(8,128)S(1)} %get-tuple-element.11.rest_5_.rest_11_), channel_id=1, source_target_pairs={{0,1},{1,0},{2,3},{3,2},{4,5},{5,4},{6,7},{7,6},{8,9},{9,8},{10,11... | collective-permute-start | bytes 147464 | tf_op jit(solution)/shard_map/ppermute | solution.py:506
  10.5 6.2 %collective-permute-start.3 = (f32[96,128]{1,0:T(8,128)S(1)}, f32[96,128]{1,0:T(8,128)S(1)}, u32[]{:S(2)}, u32[]{:S(2)}) collective-permute-start(f32[96,128]{1,0:T(8,128)S(1)} %get-tuple-element.11.rest_5_.rest_11_), channel_id=1, source_target_pairs={{0,1},{1,0},{2,4},{3,5},{4,2},{5,3},{6,7},{7,6},{8,9},{9,8},{10,12... | collective-permute-start | bytes 147464 | tf_op jit(solution)/shard_map/ppermute | solution.py:523
  10.7 6.3 %collective-permute-start.2 = (f32[96,128]{1,0:T(8,128)S(1)}, f32[96,128]{1,0:T(8,128)S(1)}, u32[]{:S(2)}, u32[]{:S(2)}) collective-permute-start(f32[96,128]{1,0:T(8,128)S(1)} %get-tuple-element.11.rest_5_.rest_11_), channel_id=1, source_target_pairs={{0,2},{2,0},{4,6},{6,4},{1,3},{3,1},{5,7},{7,5},{8,10},{10,8},{12,... | collective-permute-start | bytes 147464 | tf_op jit(solution)/shard_map/ppermute | solution.py:506
  13.5 3.5 %collective-permute-start.1 = (f32[96,128]{1,0:T(8,128)S(1)}, f32[96,128]{1,0:T(8,128)S(1)}, u32[]{:S(2)}, u32[]{:S(2)}) collective-permute-start(f32[96,128]{1,0:T(8,128)S(1)} %get-tuple-element.11.rest_5_.rest_11_), channel_id=1, source_target_pairs={{0,1},{1,0},{8,16},{9,17},{16,8},{17,9},{24,25},{25,24},{2,3},{3,2... | collective-permute-start | bytes 147464 | tf_op jit(solution)/shard_map/ppermute | solution.py:523
  13.6 5.0 %collective-permute-start = (f32[96,128]{1,0:T(8,128)S(1)}, f32[96,128]{1,0:T(8,128)S(1)}, u32[]{:S(2)}, u32[]{:S(2)}) collective-permute-start(f32[96,128]{1,0:T(8,128)S(1)} %get-tuple-element.11.rest_5_.rest_11_), channel_id=1, source_target_pairs={{0,8},{8,0},{16,24},{24,16},{1,9},{9,1},{17,25},{25,17},{2,10},{10... | collective-permute-start | bytes 147464 | tf_op jit(solution)/shard_map/ppermute | solution.py:506
  18.6 2.9 %copy-start = (s32[1536]{0:T(1024)S(1)}, s32[1536]{0:T(1024)}, u32[]{:S(2)}) copy-start(s32[1536]{0:T(1024)} %param.8) | copy-start | bytes 18436
  23.4 14.8 %all-to-all-start.1 = ((f32[32,4,128]{2,1,0:T(4,128)}), f32[32,4,128]{2,1,0:T(4,128)S(1)}, u32[]{:S(2)}, u32[]{:S(2)}) async-start(f32[32,4,128]{2,1,0:T(4,128)} %bitcast.4), calls=%async_computation.1 | async-start | bytes 131072 | tf_op jit(solution)/shard_map/all_to_all | solution.py:582
  27.1 6.4 %collective-permute-start.9 = (f32[48,128]{1,0:T(8,128)S(1)}, f32[48,128]{1,0:T(8,128)S(1)}, u32[]{:S(2)}, u32[]{:S(2)}) collective-permute-start(f32[48,128]{1,0:T(8,128)S(1)} %get-tuple-element.14.rest_5_), channel_id=1, source_target_pairs={{0,1},{1,0},{2,3},{3,2},{4,5},{5,4},{6,7},{7,6},{8,9},{9,8},{10,11... | collective-permute-start | bytes 73736 | tf_op jit(solution)/shard_map/ppermute | solution.py:506
  27.5 6.1 %collective-permute-start.8 = (f32[48,128]{1,0:T(8,128)S(1)}, f32[48,128]{1,0:T(8,128)S(1)}, u32[]{:S(2)}, u32[]{:S(2)}) collective-permute-start(f32[48,128]{1,0:T(8,128)S(1)} %get-tuple-element.14.rest_5_), channel_id=1, source_target_pairs={{0,1},{1,0},{2,4},{3,5},{4,2},{5,3},{6,7},{7,6},{8,9},{9,8},{10,12... | collective-permute-start | bytes 73736 | tf_op jit(solution)/shard_map/ppermute | solution.py:523
  27.7 5.8 %collective-permute-start.7 = (f32[48,128]{1,0:T(8,128)S(1)}, f32[48,128]{1,0:T(8,128)S(1)}, u32[]{:S(2)}, u32[]{:S(2)}) collective-permute-start(f32[48,128]{1,0:T(8,128)S(1)} %get-tuple-element.14.rest_5_), channel_id=1, source_target_pairs={{0,2},{2,0},{4,6},{6,4},{1,3},{3,1},{5,7},{7,5},{8,10},{10,8},{12,... | collective-permute-start | bytes 73736 | tf_op jit(solution)/shard_map/ppermute | solution.py:506
  30.6 3.0 %collective-permute-start.6 = (f32[48,128]{1,0:T(8,128)S(1)}, f32[48,128]{1,0:T(8,128)S(1)}, u32[]{:S(2)}, u32[]{:S(2)}) collective-permute-start(f32[48,128]{1,0:T(8,128)S(1)} %get-tuple-element.14.rest_5_), channel_id=1, source_target_pairs={{0,1},{1,0},{8,16},{9,17},{16,8},{17,9},{24,25},{25,24},{2,3},{3,2... | collective-permute-start | bytes 73736 | tf_op jit(solution)/shard_map/ppermute | solution.py:523
  30.6 4.8 %collective-permute-start.5 = (f32[48,128]{1,0:T(8,128)S(1)}, f32[48,128]{1,0:T(8,128)S(1)}, u32[]{:S(2)}, u32[]{:S(2)}) collective-permute-start(f32[48,128]{1,0:T(8,128)S(1)} %get-tuple-element.14.rest_5_), channel_id=1, source_target_pairs={{0,8},{8,0},{16,24},{24,16},{1,9},{9,1},{17,25},{25,17},{2,10},{10... | collective-permute-start | bytes 73736 | tf_op jit(solution)/shard_map/ppermute | solution.py:506

commit v3 on v2

--- a/solution.py
+++ b/solution.py
@@ -116,6 +116,8 @@
         summed = jnp.sum(both.T, axis=0, keepdims=True)
         line[k : k + 1, 0:TERMS] = summed
         line[k + 4 : k + 5, 0:TERMS] = summed
+    if copies is None:
+        return
     both = line[...]
     for at in range(devices * 4 // ROWS):
         copies[at * ROWS : (at + 1) * ROWS, :] = both
@@ -192,15 +194,8 @@
     store.wait()
 
 
-def derivative_kernel(wide, tall, deep, table):
-    lane = lax.broadcasted_iota(jnp.int32, (ROWS, LANES), 1)
-    column_x = jnp.zeros((ROWS, LANES), jnp.int32)
-    for step in range(1, wide):
-        column_x = column_x + (lane >= step * tall).astype(jnp.int32)
-    column_y = lane - column_x * tall
-    gap_x = lax.axis_index("gx") - column_x
-    gap_y = lax.axis_index("gy") - column_y
-    far = (jnp.maximum(jnp.abs(gap_x), jnp.abs(gap_y)) >= 3) & (lane < wide * tall)
+def fill_derivatives(gap_x, gap_y, known, deep, table, first, stride):
+    far = (jnp.maximum(jnp.abs(gap_x), jnp.abs(gap_y)) >= 3) & known
     weight = jnp.where(far, 1.0, 0.0)
     middle_z = slab_middle(deep)[2]
     r = (gap_x.astype(f32), gap_y.astype(f32), jnp.full((ROWS, LANES), middle_z - 0.5, f32))
@@ -226,7 +221,37 @@
                 total = total - twice * ((degree - 1.0) / degree)
             taylor[triple] = total * inverse
         scaled = taylor[triple] * weight * FACTORIAL[spot]
-        table[spot : spot + 1, :] = scaled[0:1, :]
+        table[first + spot * stride : first + spot * stride + 1, :] = scaled[0:1, :]
+
+
+def quotient(value, by, most):
+    whole = jnp.zeros(value.shape, jnp.int32)
+    for step in range(1, most):
+        whole = whole + (value >= step * by).astype(jnp.int32)
+    return whole
+
+
+def derivative_kernel(wide, tall, deep, table, pair_table):
+    columns = wide * tall
+    lane = lax.broadcasted_iota(jnp.int32, (ROWS, LANES), 1)
+    column_x = quotient(lane, tall, wide)
+    column_y = lane - column_x * tall
+    gap_x = lax.axis_index("gx") - column_x
+    gap_y = lax.axis_index("gy") - column_y
+    fill_derivatives(gap_x, gap_y, lane < columns, deep, table, 0, 1)
+    share = LANES // columns
+    local = quotient(lane, columns, share)
+    column = lane - local * columns
+    column_x = quotient(column, tall, wide)
+    column_y = column - column_x * tall
+    groups = columns // share
+    for group in range(groups):
+        domain = local + group * share
+        domain_x = quotient(domain, tall, wide)
+        domain_y = domain - domain_x * tall
+        fill_derivatives(
+            domain_x - column_x, domain_y - column_y, domain < columns, deep, pair_table, group, groups
+        )
 
 
 def split_three(value):
@@ -404,14 +429,27 @@
     lax.fori_loop(0, tiles, collect, 0, unroll=4)
 
 
-def far_kernel(tiles, wide, tall, deep, final, capacity, chosen, pack, close, received, table, *rest):
+def local_field(place, expansion, base):
+    x, y, z = place
+    over_x = None
+    for a in range(ORDER, -1, -1):
+        over_y = None
+        for b in range(ORDER - a, -1, -1):
+            over_z = None
+            for c in range(ORDER - a - b, -1, -1):
+                spot = base + PLACE[a, b, c] * ROWS
+                factor = expansion[spot : spot + ROWS, :]
+                over_z = factor if over_z is None else over_z * z + factor
+            over_y = over_z if over_y is None else over_y * y + over_z
+        over_x = over_y if over_x is None else over_x * x + over_y
+    return over_x
+
+
+def far_kernel(
+    tiles, wide, tall, deep, ghost_ids, pack, close, received, table,
+    pack_out, ghosts, speed, work, expansion, square,
+):
     columns = wide * tall
-    if final:
-        sent, moved, speed, work, expansion, square, owners, arrival = rest
-        load = pltpu.make_async_copy(chosen, owners, arrival.at[0])
-        load.start()
-    else:
-        pack_out, ghosts, leaf, speed, work, expansion, square, copies, leaving, line = rest
     row = row_ids()
     middle = slab_middle(deep)
 
@@ -437,21 +475,10 @@
         expansion[spot * ROWS : (spot + 1) * ROWS, :] = jnp.broadcast_to(summed, (ROWS, LANES))
 
     def evaluate(pair, carry):
-        x, y, z = relative_pair(pack, pair, middle)
-        over_x = None
-        for a in range(ORDER, -1, -1):
-            over_y = None
-            for b in range(ORDER - a, -1, -1):
-                over_z = None
-                for c in range(ORDER - a - b, -1, -1):
-                    spot = PLACE[a, b, c]
-                    factor = expansion[spot * ROWS : (spot + 1) * ROWS, :]
-                    over_z = factor if over_z is None else over_z * z + factor
-                over_y = over_z if over_y is None else over_y * y + over_z
-            over_x = over_y if over_x is None else over_x * x + over_y
+        total = local_field(relative_pair(pack, pair, middle), expansion, 0)
         spot = pl.multiple_of(pair * (2 * ROWS), 2 * ROWS)
-        speed[pl.ds(spot, ROWS), :] = over_x
-        speed[pl.ds(spot + ROWS, ROWS), :] = pltpu.roll(over_x, 4, 0)
+        speed[pl.ds(spot, ROWS), :] = total
+        speed[pl.ds(spot + ROWS, ROWS), :] = pltpu.roll(total, 4, 0)
         return carry
 
     lax.fori_loop(0, tiles // 2, evaluate, 0, unroll=4)
@@ -460,43 +487,124 @@
         place = pl.ds(pl.multiple_of(tile * ROWS, ROWS), ROWS)
         velocity = jnp.where(row < 3, close[place, :] + speed[place, :], 0.0)
         later = pack[place, :] + time_step * velocity
-        if final:
-            moved[place, :] = jnp.where(row < 3, later, pltpu.roll(velocity, 3, 0))
-        else:
-            pack_out[place, :] = later
+        pack_out[place, :] = later
         return carry
 
     lax.fori_loop(0, tiles, advance, 0, unroll=4)
-
-    if not final:
-        leaf_moments(pack_out, tiles, wide * tall * deep, copies, work, line)
-        store = pltpu.make_async_copy(copies, leaf, leaving.at[0])
-        store.start()
-        pick_positions(pack_out, tiles, chosen, ghosts)
-        store.wait()
-        return
-
-    group = wide * tall
+    pick_positions(pack_out, tiles, ghost_ids, ghosts)
+
+
+def moments_kernel(tiles, pack, line, work):
+    leaf_moments(pack, tiles, 0, None, work, line)
+
+
+def handover_kernel(tiles, group, capacity, owners_in, pack, close, line, sent, owners, arrival):
+    load = pltpu.make_async_copy(owners_in, owners, arrival.at[0])
+    load.start()
     load.wait()
     placer = block_placer(owners, group, capacity)
+    size = 6 * capacity + 4
+    slot = lax.broadcasted_iota(jnp.int32, (group * capacity, LANES), 0)
+    lane = lax.broadcasted_iota(jnp.int32, (group * capacity, LANES), 1)
+    filled = jnp.sum(placer.astype(f32), axis=1, keepdims=True)
+    filled = jnp.where(lane == lax.rem(slot, capacity), filled, 0.0)
     placer = jnp.concatenate([placer] * 3, axis=1)
+    row = row_ids()
+    column = jnp.where(row < 3, line[...], 0.0)[0:4, :]
+    for owner in range(group):
+        base = owner * size + 6 * capacity
+        sent[base : base + 3, :] = column[0:3, :]
+        slots = filled[owner * capacity : (owner + 1) * capacity, :]
+        sent[base + 3 : base + 4, :] = jnp.sum(slots, axis=0, keepdims=True)
     for field in range(6):
-        values = split_three(moved[pl.ds(field, tiles, stride=ROWS), :])
-        values = jnp.concatenate([value.astype(bf16) for value in values], axis=0)
+        values = (pack if field < 3 else close)[pl.ds(field % 3, tiles, stride=ROWS), :]
+        values = jnp.concatenate([value.astype(bf16) for value in split_three(values)], axis=0)
         placed = jnp.dot(placer, values, preferred_element_type=f32)
         for owner in range(group):
-            base = (owner * 6 + field) * capacity
+            base = owner * size + field * capacity
             sent[base : base + capacity, :] = placed[owner * capacity : (owner + 1) * capacity, :]
 
 
-def receive_kernel(capacity, handed, positions, velocity):
-    for sender in range(positions.shape[1] // capacity):
-        slots = slice(sender * capacity, (sender + 1) * capacity)
-        for axis in range(3):
-            base = (sender * 6 + axis) * capacity
-            positions[axis, slots, :] = handed[base : base + capacity, :]
-            base = base + 3 * capacity
-            velocity[axis, slots, :] = handed[base : base + capacity, :]
+def finish_kernel(wide, tall, deep, capacity, handed, table, positions, velocity, work, sums, expansion, square):
+    columns = wide * tall
+    size = 6 * capacity + 4
+    share = LANES // columns
+    groups = columns // share
+    row = row_ids()
+    lane = lax.broadcasted_iota(jnp.int32, (ROWS, LANES), 1)
+    low = row < 4
+    part = jnp.where(low, row, row - 4)
+    work[...] = jnp.zeros_like(work)
+    for k in range(3):
+        total = handed[pl.ds(6 * capacity + k, columns, stride=size), :]
+        for copy in range(share):
+            square[copy * columns : (copy + 1) * columns, :] = total
+        turned = square[...].T[0:TERMS, :]
+        work[pl.ds(k, TERMS, stride=ROWS), :] = turned
+        work[pl.ds(k + 4, TERMS, stride=ROWS), :] = turned
+
+    def expand(group, carry):
+        for spot, outer in enumerate(POWERS):
+            total = None
+            for inner_spot, inner in enumerate(POWERS):
+                if sum(outer) + sum(inner) > ORDER:
+                    continue
+                merged = tuple(o + i for o, i in zip(outer, inner))
+                factor = spread(table, PLACE[merged] * groups + group)
+                term = factor * work[inner_spot * ROWS : (inner_spot + 1) * ROWS, :]
+                total = term if total is None else total + term
+            step = columns // 2
+            while step:
+                total = total + pltpu.roll(total, LANES - step, 1)
+                step //= 2
+            at = (group * TERMS + spot) * ROWS
+            sums[pl.ds(pl.multiple_of(at, ROWS), ROWS), :] = total * (1.0 / FACTORIAL[spot])
+        return carry
+
+    lax.fori_loop(0, groups, expand, 0)
+    reached = [
+        sender
+        for sender in range(columns)
+        if max(sender // tall, wide - 1 - sender // tall, sender % tall, tall - 1 - sender % tall) >= 3
+    ]
+    for sender in reached:
+        group, local = divmod(sender, share)
+        for spot in range(TERMS):
+            at = (sender * TERMS + spot) * ROWS
+            value = sums[(group * TERMS + spot) * ROWS : (group * TERMS + spot + 1) * ROWS, :]
+            expansion[at : at + ROWS, :] = jnp.broadcast_to(
+                value[:, local * columns : local * columns + 1], (ROWS, LANES)
+            )
+    middle_z = slab_middle(deep)[2]
+    for sender in range(columns):
+        middle = (sender // tall + 0.5, sender % tall + 0.5, middle_z)
+        base = sender * size
+        flags = spread(handed, base + 6 * capacity + 3)
+        for first in range(0, capacity, 2):
+            fields = [
+                jnp.where(
+                    low,
+                    spread(handed, base + field * capacity + first),
+                    spread(handed, base + field * capacity + first + 1),
+                )
+                for field in range(6)
+            ]
+            here = jnp.where(part == 0, fields[0], jnp.where(part == 1, fields[1], fields[2]))
+            close = jnp.where(part == 0, fields[3], jnp.where(part == 1, fields[4], fields[5]))
+            place = [fields[axis] - middle[axis] for axis in range(3)]
+            speed = close
+            if sender in reached:
+                speed = speed + local_field(place, expansion, sender * TERMS * ROWS)
+            picked = jnp.where(lane == jnp.where(low, first, first + 1), flags, 0.0)
+            there = jnp.sum(picked, axis=1, keepdims=True) > 0.5
+            speed = jnp.where(there, speed, 0.0)
+            later = jnp.where(there, here + time_step * speed, 0.0)
+            for half in range(2):
+                slot = sender * capacity + first + half
+                for axis in range(3):
+                    at = 4 * half + axis
+                    positions[axis, slot : slot + 1, :] = later[at : at + 1, :]
+                    velocity[axis, slot : slot + 1, :] = speed[at : at + 1, :]
 
 
 def even_pairs(block, name):
@@ -543,6 +651,16 @@
     in_hbm = functools.partial(pltpu.with_memory_space_constraint, memory_space=pltpu.HBM)
 
     copies = pltpu.VMEM((devices * 4, LANES), f32)
+    square = pltpu.VMEM((LANES, LANES), f32)
+    gather_moments = pl.pallas_call(
+        functools.partial(moments_kernel, tiles),
+        out_shape=jax.ShapeDtypeStruct((ROWS, LANES), f32),
+        in_specs=[in_vmem],
+        out_specs=in_vmem,
+        scratch_shapes=[work],
+        compiler_params=params,
+        name="moments",
+    )
     one_copy = pltpu.SemaphoreType.DMA((1,))
 
     pack, ghosts, leaf = pl.pallas_call(
@@ -563,10 +681,13 @@
         compiler_params=params,
         name="prologue",
     )(in_hbm(offsets), in_hbm(strength), in_hbm(ghost_ids))
-    table = pl.pallas_call(
+    table, pair_table = pl.pallas_call(
         functools.partial(derivative_kernel, wide, tall, deep),
-        out_shape=jax.ShapeDtypeStruct((TERMS, LANES), f32),
-        out_specs=in_vmem,
+        out_shape=(
+            jax.ShapeDtypeStruct((TERMS, LANES), f32),
+            jax.ShapeDtypeStruct((TERMS * (group * group // LANES), LANES), f32),
+        ),
+        out_specs=(in_vmem,) * 2,
         compiler_params=params,
         name="derivatives",
     )()
@@ -579,7 +700,11 @@
             arrived.extend((even_pairs(ghosts, name), odd_pairs(ghosts, name)))
         if not final:
             strengths = arrived
-        received = lax.all_to_all(leaf, everywhere, split_axis=0, concat_axis=0, tiled=True)
+        if final:
+            slab = gather_moments(pack)
+            column = slab + even_pairs(slab, "gz") if deep == 2 else lax.psum(slab, "gz")
+        else:
+            received = lax.all_to_all(leaf, everywhere, split_axis=0, concat_axis=0, tiled=True)
         close = pl.pallas_call(
             functools.partial(near_kernel, tiles, ghost_tiles, deep, beside),
             out_shape=pack_type,
@@ -597,42 +722,43 @@
             compiler_params=params,
             name="near",
         )(in_hbm(pair_targets), in_hbm(pair_sources), pack, *arrived, *strengths)
-        speed, square = pltpu.VMEM((tiles * ROWS, LANES), f32), pltpu.VMEM((LANES, LANES), f32)
-        if final:
-            chosen = in_hbm(owners.reshape(1, tiles))
-            out_shape = jax.ShapeDtypeStruct((group * capacity * 6, LANES), f32)
-            out_specs = in_vmem
-            extra = [
-                pltpu.VMEM((tiles * ROWS, LANES), f32), speed, work, work, square,
-                pltpu.VMEM((1, tiles), jnp.int32), one_copy,
-            ]
-        else:
-            chosen = ghost_ids
+        if not final:
             half_type = jax.ShapeDtypeStruct((ghost_tiles * 4, LANES), f32)
-            out_shape = (pack_type, half_type, leaf_type)
-            out_specs = (in_vmem, in_vmem, in_place)
-            extra = [speed, work, work, square, copies, one_copy, line]
-        result = pl.pallas_call(
-            functools.partial(far_kernel, tiles, wide, tall, deep, final, capacity),
-            out_shape=out_shape,
-            in_specs=[in_place if final else in_vmem] + [in_vmem] * 4,
-            out_specs=out_specs,
-            scratch_shapes=extra,
-            compiler_params=params,
-            name="last_far" if final else "far",
-        )(chosen, pack, close, received, table)
-        if not final:
-            pack, ghosts, leaf = result
-    handed = lax.all_to_all(result, ("gx", "gy"), split_axis=0, concat_axis=0, tiled=True)
+            pack, ghosts = pl.pallas_call(
+                functools.partial(far_kernel, tiles, wide, tall, deep),
+                out_shape=(pack_type, half_type),
+                in_specs=[in_vmem] * 5,
+                out_specs=(in_vmem,) * 2,
+                scratch_shapes=[pltpu.VMEM((tiles * ROWS, LANES), f32), work, work, square],
+                compiler_params=params,
+                name="far",
+            )(ghost_ids, pack, close, received, table)
+    size = 6 * capacity + 4
+    sent = pl.pallas_call(
+        functools.partial(handover_kernel, tiles, group, capacity),
+        out_shape=jax.ShapeDtypeStruct((group * size, LANES), f32),
+        in_specs=[in_place] + [in_vmem] * 3,
+        out_specs=in_vmem,
+        scratch_shapes=[pltpu.VMEM((1, tiles), jnp.int32), one_copy],
+        compiler_params=params,
+        name="handover",
+    )(in_hbm(owners.reshape(1, tiles)), pack, close, column)
+    handed = lax.all_to_all(sent, ("gx", "gy"), split_axis=0, concat_axis=0, tiled=True)
     moved = jax.ShapeDtypeStruct((3, group * capacity, LANES), f32)
     moved = pl.pallas_call(
-        functools.partial(receive_kernel, capacity),
+        functools.partial(finish_kernel, wide, tall, deep, capacity),
         out_shape=(moved, moved),
-        in_specs=[in_vmem],
+        in_specs=[in_vmem] * 2,
         out_specs=(in_vmem,) * 2,
+        scratch_shapes=[
+            work,
+            pltpu.VMEM((group * group // LANES * TERMS * ROWS, LANES), f32),
+            pltpu.VMEM((group * TERMS * ROWS, LANES), f32),
+            square,
+        ],
         compiler_params=params,
-        name="receive",
-    )(handed)
+        name="finish",
+    )(handed, pair_table)
     return tuple(value.transpose(1, 0, 2) for value in moved)
 
 

time: 52.8 us -> 50.2 us (0.951)
  starting transfers between devices: 23.8 us -> 18.7 us
  Pallas kernels: 11.6 us -> 13.7 us
    all_to_all x2 -> x1, starting transfers between devices: 11.1 us -> 7.33 us  [per_device(): lax.all_to_all(leaf, everywhere, split_axis=0, concat_axis=0, tiled=True)]
    pallas_call x3 -> x4, Pallas kernels: 3.65 us -> 5.61 us  [the longest x1 2.8 us: per_device(): pl.pallas_call(functools.partial(finish_kernel, wide, tall, deep, capacit...]
    ppermute x6 -> x7, starting transfers between devices: 12.2 us -> 11 us  [even_pairs(): return lax.ppermute(block, name, [(i, i ^ 1) for i in range(count)])]
    all_to_all x1, blocking collectives: 12.6 us -> 13.1 us  [per_device(): lax.all_to_all(sent, ('gx', 'gy'), split_axis=0, concat_axis=0, tiled=True)]
    ppermute x6 -> x7, waiting for transfers between devices: 3.74 us -> 3.59 us  [even_pairs(): return lax.ppermute(block, name, [(i, i ^ 1) for i in range(count)])]
  transfers between devices with their start and end apart: 12 -> 12, of which waited for: 3 -> 3; matrix products, arithmetic and copies ran while one was open for 0% -> 0% of each run, Pallas kernels for 11% -> 6%
where the time goes in v3:
time: 50.2 us; the launch traced here: 49.9 us
  starting transfers between devices  18.7 us (37%)
  Pallas kernels  13.7 us (27%)
  blocking collectives  13.1 us (26%)
  waiting for transfers between devices  3.6 us (7%)
  between operations  0.76 us (2%)
    all_to_all x1, blocking collectives, per_device(): lax.all_to_all(sent, ('gx', 'gy'), split_axis=0, concat_axis=0, tiled=True)  13.1 us
    ppermute x7, starting transfers between devices, even_pairs(): return lax.ppermute(block, name, [(i, i ^ 1) for i in range(count)])  11 us
    all_to_all x1, starting transfers between devices, per_device(): lax.all_to_all(leaf, everywhere, split_axis=0, concat_axis=0, tiled=True)  7.33 us
    pallas_call x2, Pallas kernels, per_device(): pl.pallas_call(functools.partial(near_kernel, tiles, ghost_tiles, deep, b...  5.72 us
    ppermute x7, waiting for transfers between devices, even_pairs(): return lax.ppermute(block, name, [(i, i ^ 1) for i in range(count)])  3.59 us
    pallas_call x1, Pallas kernels, per_device(): pl.pallas_call(functools.partial(finish_kernel, wide, tall, deep, capacit...  2.8 us
    pallas_call x1, Pallas kernels, per_device(): pl.pallas_call(functools.partial(prologue_kernel, tiles, devices, deep),...  2.16 us
    pallas_call x1, Pallas kernels, per_device(): pl.pallas_call(functools.partial(far_kernel, tiles, wide, tall, deep), ou...  1.26 us
  transfers between devices with their start and end apart: 12, of which 3 were waited for; matrix products, arithmetic and copies ran while one was open for 0% of the time, Pallas kernels for 6%

profile of v3, /device:TPU:0, one launch (start us, length us, event | category | flops | bytes accessed | tf_op | source)
XLA Modules:
  0.0 49.9 jit_solution(11896012093204422318)
XLA Ops:
  0.6 2.2 %prologue.1 = (f32[256,128]{1,0:T(8,128)S(1)}, f32[96,128]{1,0:T(8,128)S(1)}, f32[128,128]{1,0:T(8,128)}) custom-call(f32[3,4096]{1,0:T(4,128)} %offsets_in.1, f32[3,4096]{1,0:T(4,128)} %strength_in.1, s32[12,128]{1,0:T(8,128)} %bitcast.7), custom_call_target="tpu_custom_call" | custom-call | tf_op jit(solution)/shard_map/prologue/pallas_call | solution.py:666
  2.8 7.3 %all-to-all-start = ((f32[32,4,128]{2,1,0:T(4,128)}), f32[32,4,128]{2,1,0:T(4,128)S(1)}, u32[]{:S(2)}, u32[]{:S(2)}) async-start(f32[32,4,128]{2,1,0:T(4,128)} %bitcast.2), calls=%async_computation | async-start | bytes 131072 | tf_op jit(solution)/shard_map/all_to_all | solution.py:707
  10.1 0.3 collective-permute-start.4
  10.5 0.3 collective-permute-start.3
  10.7 2.8 %collective-permute-start.2 = (f32[96,128]{1,0:T(8,128)S(1)}, f32[96,128]{1,0:T(8,128)S(1)}, u32[]{:S(2)}, u32[]{:S(2)}) collective-permute-start(f32[96,128]{1,0:T(8,128)S(1)} %get-tuple-element.12.rest_5_.rest_11_), channel_id=1, source_target_pairs={{0,2},{2,0},{4,6},{6,4},{1,3},{3,1},{5,7},{7,5},{8,10},{10,8},{12,... | collective-permute-start | bytes 147464 | tf_op jit(solution)/shard_map/ppermute | solution.py:614
  13.5 0.0 collective-permute-start.1
  13.6 3.0 %collective-permute-start = (f32[96,128]{1,0:T(8,128)S(1)}, f32[96,128]{1,0:T(8,128)S(1)}, u32[]{:S(2)}, u32[]{:S(2)}) collective-permute-start(f32[96,128]{1,0:T(8,128)S(1)} %get-tuple-element.12.rest_5_.rest_11_), channel_id=1, source_target_pairs={{0,8},{8,0},{16,24},{24,16},{1,9},{9,1},{17,25},{25,17},{2,10},{10... | collective-permute-start | bytes 147464 | tf_op jit(solution)/shard_map/ppermute | solution.py:614
  16.5 0.2 derivatives.1
  16.7 0.0 collective-permute-done.4.rest_4_.rest_10_
  16.7 0.0 collective-permute-done.3.rest_3_.rest_9_
  16.8 0.3 collective-permute-done.2.rest_2_.rest_8_
  17.0 0.0 collective-permute-done.1.rest_1_.rest_7_
  17.0 1.5 %collective-permute-done.rest_0_.rest_6_ = f32[96,128]{1,0:T(8,128)S(1)} collective-permute-done((f32[96,128]{1,0:T(8,128)S(1)}, f32[96,128]{1,0:T(8,128)S(1)}, u32[]{:S(2)}, u32[]{:S(2)}) %collective-permute-start) | collective-permute-done | bytes 49184 | tf_op jit(solution)/shard_map/ppermute | solution.py:614
  18.6 2.9 %near.2.close = f32[256,128]{1,0:T(8,128)S(1)} custom-call(s32[128]{0:T(128)} %targets_in.3, s32[128]{0:T(128)} %sources_in.3, f32[256,128]{1,0:T(8,128)S(1)} %get-tuple-element.11.pack, f32[96,128]{1,0:T(8,128)S(1)} %collective-permute-done.rest_0_.rest_6_, f32[96,128]{1,0:T(8,128)S(1)} %collective-permute-done.1.rest_1_.rest_7_, ...), custom_call_target="tpu_custom_call" | custom-call | tf_op jit(solution)/shard_map/near/pallas_call | solution.py:708
  21.4 0.0 all-to-all-done
  21.5 1.3 %far.1 = (f32[256,128]{1,0:T(8,128)S(1)}, f32[48,128]{1,0:T(8,128)S(1)}) custom-call(s32[12,128]{1,0:T(8,128)S(1)} %bitcast.8, f32[256,128]{1,0:T(8,128)S(1)} %get-tuple-element.11.pack, f32[256,128]{1,0:T(8,128)S(1)} %near.2.close, f32[128,128]{1,0:T(8,128)S(1)} %bitcast.6, f32[56,128]{1,0:T(8,128)S(1)} %get-tuple-element.14.table), custom_call_target="tpu_custom_call" | custom-call | tf_op jit(solution)/shard_map/far/pallas_call | solution.py:727
  22.7 0.5 %moments.1 = f32[8,128]{1,0:T(8,128)S(1)} custom-call(f32[256,128]{1,0:T(8,128)S(1)} %get-tuple-element.15.pack), custom_call_target="tpu_custom_call" | custom-call | tf_op jit(solution)/shard_map/moments/pallas_call | solution.py:704
  23.3 0.1 collective-permute-start.10
  23.3 0.5 collective-permute-start.9
  23.8 0.1 collective-permute-start.8
  23.9 1.8 %collective-permute-start.7 = (f32[48,128]{1,0:T(8,128)S(1)}, f32[48,128]{1,0:T(8,128)S(1)}, u32[]{:S(2)}, u32[]{:S(2)}) collective-permute-start(f32[48,128]{1,0:T(8,128)S(1)} %get-tuple-element.16.rest_5_), channel_id=1, source_target_pairs={{0,2},{2,0},{4,6},{6,4},{1,3},{3,1},{5,7},{7,5},{8,10},{10,8},{12,... | collective-permute-start | bytes 73736 | tf_op jit(solution)/shard_map/ppermute | solution.py:614
  25.7 0.0 collective-permute-start.6
  25.7 0.0 collective-permute-done.10
  25.7 2.6 %collective-permute-start.5 = (f32[48,128]{1,0:T(8,128)S(1)}, f32[48,128]{1,0:T(8,128)S(1)}, u32[]{:S(2)}, u32[]{:S(2)}) collective-permute-start(f32[48,128]{1,0:T(8,128)S(1)} %get-tuple-element.16.rest_5_), channel_id=1, source_target_pairs={{0,8},{8,0},{16,24},{24,16},{1,9},{9,1},{17,25},{25,17},{2,10},{10... | collective-permute-start | bytes 73736 | tf_op jit(solution)/shard_map/ppermute | solution.py:614
  28.3 0.0 collective-permute-done.9.rest_4_
  28.3 0.0 collective-permute-done.8.rest_3_
  28.3 0.0 collective-permute-done.6.rest_1_
  28.3 1.8 %collective-permute-done.5.rest_0_ = f32[48,128]{1,0:T(8,128)S(1)} collective-permute-done((f32[48,128]{1,0:T(8,128)S(1)}, f32[48,128]{1,0:T(8,128)S(1)}, u32[]{:S(2)}, u32[]{:S(2)}) %collective-permute-start.5) | collective-permute-done | bytes 24608 | tf_op jit(solution)/shard_map/ppermute | solution.py:614
  30.1 2.9 %near.3.close = f32[256,128]{1,0:T(8,128)S(1)} custom-call(s32[128]{0:T(128)} %targets_in.3, s32[128]{0:T(128)} %sources_in.3, f32[256,128]{1,0:T(8,128)S(1)} %get-tuple-element.15.pack, f32[48,128]{1,0:T(8,128)S(1)} %collective-permute-done.5.rest_0_, f32[48,128]{1,0:T(8,128)S(1)} %collective-permute-done.6.rest_1_, ...), custom_call_target="tpu_custom_call" | custom-call | tf_op jit(solution)/shard_map/near/pallas_call | solution.py:708
  33.0 1.0 %handover.1 = f32[448,128]{1,0:T(8,128)S(1)} custom-call(s32[1,32]{1,0:T(1,128)} %bitcast.9, f32[256,128]{1,0:T(8,128)S(1)} %get-tuple-element.15.pack, f32[256,128]{1,0:T(8,128)S(1)} %near.3.close, f32[8,128]{1,0:T(8,128)S(1)} %add.3.line), custom_call_target="tpu_custom_call" | custom-call | tf_op jit(solution)/shard_map/handover/pallas_call | solution.py:737
  34.0 13.1 %all_to_all.22 = f32[16,28,128]{2,1,0:T(8,128)S(1)} all-to-all(f32[16,28,128]{2,1,0:T(8,128)S(1)} %all_to_all.17), channel_id=1, replica_groups=mesh['gx'=4,'gy'=4,'gz'=2] {'gx','gy'}, dimensions={0} | all-to-all | bytes 458752 | tf_op jit(solution)/shard_map/all_to_all | solution.py:746
  47.1 2.8 %finish.1 = (f32[3,64,128]{2,1,0:T(8,128)}, f32[3,64,128]{2,1,0:T(8,128)}) custom-call(f32[448,128]{1,0:T(8,128)S(1)} %all_to_all.19.handed, f32[112,128]{1,0:T(8,128)S(1)} %get-tuple-element.17.table), custom_call_target="tpu_custom_call" | custom-call | tf_op jit(solution)/shard_map/finish/pallas_call | solution.py:748
  (6 shorter events, 0.0 us)
Async XLA Ops:
  2.8 18.6 %all-to-all-start = ((f32[32,4,128]{2,1,0:T(4,128)}), f32[32,4,128]{2,1,0:T(4,128)S(1)}, u32[]{:S(2)}, u32[]{:S(2)}) async-start(f32[32,4,128]{2,1,0:T(4,128)} %bitcast.2), calls=%async_computation | async-start | bytes 131072 | tf_op jit(solution)/shard_map/all_to_all | solution.py:707
  10.1 6.6 %collective-permute-start.4 = (f32[96,128]{1,0:T(8,128)S(1)}, f32[96,128]{1,0:T(8,128)S(1)}, u32[]{:S(2)}, u32[]{:S(2)}) collective-permute-start(f32[96,128]{1,0:T(8,128)S(1)} %get-tuple-element.12.rest_5_.rest_11_), channel_id=1, source_target_pairs={{0,1},{1,0},{2,3},{3,2},{4,5},{5,4},{6,7},{7,6},{8,9},{9,8},{10,11... | collective-permute-start | bytes 147464 | tf_op jit(solution)/shard_map/ppermute | solution.py:614
  10.5 6.3 %collective-permute-start.3 = (f32[96,128]{1,0:T(8,128)S(1)}, f32[96,128]{1,0:T(8,128)S(1)}, u32[]{:S(2)}, u32[]{:S(2)}) collective-permute-start(f32[96,128]{1,0:T(8,128)S(1)} %get-tuple-element.12.rest_5_.rest_11_), channel_id=1, source_target_pairs={{0,1},{1,0},{2,4},{3,5},{4,2},{5,3},{6,7},{7,6},{8,9},{9,8},{10,12... | collective-permute-start | bytes 147464 | tf_op jit(solution)/shard_map/ppermute | solution.py:631
  10.7 6.3 %collective-permute-start.2 = (f32[96,128]{1,0:T(8,128)S(1)}, f32[96,128]{1,0:T(8,128)S(1)}, u32[]{:S(2)}, u32[]{:S(2)}) collective-permute-start(f32[96,128]{1,0:T(8,128)S(1)} %get-tuple-element.12.rest_5_.rest_11_), channel_id=1, source_target_pairs={{0,2},{2,0},{4,6},{6,4},{1,3},{3,1},{5,7},{7,5},{8,10},{10,8},{12,... | collective-permute-start | bytes 147464 | tf_op jit(solution)/shard_map/ppermute | solution.py:614
  13.5 3.5 %collective-permute-start.1 = (f32[96,128]{1,0:T(8,128)S(1)}, f32[96,128]{1,0:T(8,128)S(1)}, u32[]{:S(2)}, u32[]{:S(2)}) collective-permute-start(f32[96,128]{1,0:T(8,128)S(1)} %get-tuple-element.12.rest_5_.rest_11_), channel_id=1, source_target_pairs={{0,1},{1,0},{8,16},{9,17},{16,8},{17,9},{24,25},{25,24},{2,3},{3,2... | collective-permute-start | bytes 147464 | tf_op jit(solution)/shard_map/ppermute | solution.py:631
  13.6 5.0 %collective-permute-start = (f32[96,128]{1,0:T(8,128)S(1)}, f32[96,128]{1,0:T(8,128)S(1)}, u32[]{:S(2)}, u32[]{:S(2)}) collective-permute-start(f32[96,128]{1,0:T(8,128)S(1)} %get-tuple-element.12.rest_5_.rest_11_), channel_id=1, source_target_pairs={{0,8},{8,0},{16,24},{24,16},{1,9},{9,1},{17,25},{25,17},{2,10},{10... | collective-permute-start | bytes 147464 | tf_op jit(solution)/shard_map/ppermute | solution.py:614
  18.6 2.9 %copy-start = (s32[1536]{0:T(1024)S(1)}, s32[1536]{0:T(1024)}, u32[]{:S(2)}) copy-start(s32[1536]{0:T(1024)} %param.8) | copy-start | bytes 18436
  23.3 2.4 %collective-permute-start.10 = (f32[8,128]{1,0:T(8,128)S(1)}, f32[8,128]{1,0:T(8,128)S(1)}, u32[]{:S(2)}, u32[]{:S(2)}) collective-permute-start(f32[8,128]{1,0:T(8,128)S(1)} %moments.1), channel_id=1, source_target_pairs={{0,1},{1,0},{2,3},{3,2},{4,5},{5,4},{6,7},{7,6},{8,9},{9,8},{10,11... | collective-permute-start | bytes 12296 | tf_op jit(solution)/shard_map/ppermute | solution.py:614
  23.3 4.9 %collective-permute-start.9 = (f32[48,128]{1,0:T(8,128)S(1)}, f32[48,128]{1,0:T(8,128)S(1)}, u32[]{:S(2)}, u32[]{:S(2)}) collective-permute-start(f32[48,128]{1,0:T(8,128)S(1)} %get-tuple-element.16.rest_5_), channel_id=1, source_target_pairs={{0,1},{1,0},{2,3},{3,2},{4,5},{5,4},{6,7},{7,6},{8,9},{9,8},{10,11... | collective-permute-start | bytes 73736 | tf_op jit(solution)/shard_map/ppermute | solution.py:614
  23.8 4.4 %collective-permute-start.8 = (f32[48,128]{1,0:T(8,128)S(1)}, f32[48,128]{1,0:T(8,128)S(1)}, u32[]{:S(2)}, u32[]{:S(2)}) collective-permute-start(f32[48,128]{1,0:T(8,128)S(1)} %get-tuple-element.16.rest_5_), channel_id=1, source_target_pairs={{0,1},{1,0},{2,4},{3,5},{4,2},{5,3},{6,7},{7,6},{8,9},{9,8},{10,12... | collective-permute-start | bytes 73736 | tf_op jit(solution)/shard_map/ppermute | solution.py:631
  23.9 4.4 %collective-permute-start.7 = (f32[48,128]{1,0:T(8,128)S(1)}, f32[48,128]{1,0:T(8,128)S(1)}, u32[]{:S(2)}, u32[]{:S(2)}) collective-permute-start(f32[48,128]{1,0:T(8,128)S(1)} %get-tuple-element.16.rest_5_), channel_id=1, source_target_pairs={{0,2},{2,0},{4,6},{6,4},{1,3},{3,1},{5,7},{7,5},{8,10},{10,8},{12,... | collective-permute-start | bytes 73736 | tf_op jit(solution)/shard_map/ppermute | solution.py:614
  25.7 2.6 %collective-permute-start.6 = (f32[48,128]{1,0:T(8,128)S(1)}, f32[48,128]{1,0:T(8,128)S(1)}, u32[]{:S(2)}, u32[]{:S(2)}) collective-permute-start(f32[48,128]{1,0:T(8,128)S(1)} %get-tuple-element.16.rest_5_), channel_id=1, source_target_pairs={{0,1},{1,0},{8,16},{9,17},{16,8},{17,9},{24,25},{25,24},{2,3},{3,2... | collective-permute-start | bytes 73736 | tf_op jit(solution)/shard_map/ppermute | solution.py:631
  25.7 4.4 %collective-permute-start.5 = (f32[48,128]{1,0:T(8,128)S(1)}, f32[48,128]{1,0:T(8,128)S(1)}, u32[]{:S(2)}, u32[]{:S(2)}) collective-permute-start(f32[48,128]{1,0:T(8,128)S(1)} %get-tuple-element.16.rest_5_), channel_id=1, source_target_pairs={{0,8},{8,0},{16,24},{24,16},{1,9},{9,1},{17,25},{25,17},{2,10},{10... | collective-permute-start | bytes 73736 | tf_op jit(solution)/shard_map/ppermute | solution.py:614
